TPU v7x, 32 devices: a whole 2x2x4 slice. The times are simulated.
32 devices in a mesh: groups: 2 (over x), blk: 16 (over z, y, core).
Axes of the slice: x: 2, y: 2, z: 4, core: 2. Of those that a mesh axis runs over, the one named last changes fastest.
Arguments:
- query_inputs: bfloat16 [8192, 4096], P(('groups', 'blk')), parts along dimension 0, may hold values from -6 to 6
- query_grads: bfloat16 [8192, 4096], P(('groups', 'blk')), parts along dimension 0, may hold values from -6 to 6
- proj_in: bfloat16 [4096, 64], replicated, may hold values from -0.09375 to 0.09375
- proj_out: bfloat16 [4096, 64], replicated, may hold values from -0.09375 to 0.09375
- train_rows: bfloat16 [8192, 4096], P(('groups', 'blk')), parts along dimension 0, may hold values from -0.09375 to 0.09375
- token_owner: int32 [8192, 1], P(('groups', 'blk')), parts along dimension 0, may hold values from 0 to 15; in each aligned block of 256 rows (0 to 255, 256 to 511, ...) at most 64 rows name the same one
- token_slot: int32 [8192], P(('groups', 'blk')), parts along dimension 0, may hold values from 0 to 31
Outputs:
- influence: bfloat16 [12, 32, 8192], P(None, None, ('groups', 'blk')), parts along dimension 2
There are 2 independent parts, one for each index of `groups`. A program takes and returns all parts, laid end to end along the dimension named above; an argument that names none is the same for every part. Nothing has to cross between parts.
Inputs may be any that keep to these rules, and one draw needn't show every extreme that they name: `token_owner`: within the tokens of one device no owner is named by more than 64 tokens, a bound that some block reaches.
All inputs are finite; a program needn't handle non-finite values. Where the computation divides by a largest or mean magnitude, that divisor is 1e-20 or more.
Results may differ from a plain program's by a relative error of at most 0.0069.
Values may be sent and summed in bfloat16 or wider, within the bound.
A program may use at most 64 MiB of HBM per device.

v0:
```python
import jax
import jax.numpy as jnp
from jax import lax
from jax.sharding import PartitionSpec as P

DOC_DEV = 32
STOPS = 12
NEWTON_STEPS = 6
LEAD = 5


HIGHEST_PRECISION = lax.Precision.HIGHEST


def passed_along(value, axis, steps):
    count = lax.axis_size(axis)
    pairs = [(source, (source + steps) % count) for source in range(count)]
    return lax.ppermute(value, axis, pairs)


def inverse_factor(gram_sum, counts):
    width_low = gram_sum.shape[1]
    identity_mat = jnp.eye(width_low, dtype=jnp.float32)
    damped = gram_sum / (counts[:, None, None] + 1.0) + identity_mat[None]
    row_bound = jnp.max(jnp.sum(jnp.abs(damped), axis=2), axis=1)
    approx = identity_mat[None] / row_bound[:, None, None]
    for iteration in range(NEWTON_STEPS):
        product = jnp.einsum("dab,dbc->dac", damped, approx, precision=HIGHEST_PRECISION)
        approx = jnp.einsum(
            "dab,dbc->dac", approx, 2.0 * identity_mat[None] - product, precision=HIGHEST_PRECISION
        )
    return approx


def local(query_inputs, query_grads, proj_in, proj_out, train_rows, token_owner, token_slot):
    tok_count = query_inputs.shape[0]
    width_low = proj_in.shape[1]
    owners = lax.axis_size("blk")
    capacity = 4 * tok_count // owners
    grads_low = jnp.dot(query_grads, proj_out, preferred_element_type=jnp.float32).astype(
        jnp.bfloat16
    )
    inputs_low = jnp.dot(query_inputs, proj_in, preferred_element_type=jnp.float32).astype(
        jnp.bfloat16
    )
    low_rows = jnp.concatenate([grads_low, inputs_low], axis=1)
    owner_ids = token_owner[:, 0]
    owner_hot = (owner_ids[:, None] == jnp.arange(owners, dtype=jnp.int32)[None, :]).astype(
        jnp.float32
    )
    tok_index = jnp.arange(tok_count, dtype=jnp.int32)
    earlier = (tok_index[:, None] > tok_index[None, :]).astype(jnp.float32)
    before = jnp.dot(earlier, owner_hot, precision=HIGHEST_PRECISION)
    rank_in = jnp.sum(before * owner_hot, axis=1).astype(jnp.int32)
    position = owner_ids * capacity + rank_in
    slot_index = jnp.arange(owners * capacity, dtype=jnp.int32)
    placed = slot_index[:, None] == position[None, :]
    send_rows = jnp.dot(
        placed.astype(jnp.bfloat16), low_rows, preferred_element_type=jnp.float32
    ).astype(jnp.bfloat16)
    send_slot = jnp.sum(jnp.where(placed, token_slot[None, :] + 1, 0), axis=1)
    recv_rows, recv_slot = (
        lax.all_to_all(
            send_rows.reshape(owners, capacity, 2 * width_low),
            "blk",
            split_axis=0,
            concat_axis=0,
            tiled=True,
        ),
        lax.all_to_all(
            send_slot.reshape(owners, capacity), "blk", split_axis=0, concat_axis=0, tiled=True
        ),
    )
    recv_rows = recv_rows.reshape(owners * capacity, 2 * width_low)
    recv_slot = recv_slot.reshape(owners * capacity)
    doc_index = jnp.arange(1, DOC_DEV + 1, dtype=jnp.int32)
    doc_hot = recv_slot[:, None] == doc_index[None, :]
    counts = jnp.sum(doc_hot.astype(jnp.float32), axis=0)
    hot_bf = doc_hot.astype(jnp.bfloat16)
    grads_recv = recv_rows[:, :width_low]
    inputs_recv = recv_rows[:, width_low:]
    spread_grads = (hot_bf[:, :, None] * grads_recv[:, None, :]).reshape(
        owners * capacity, DOC_DEV * width_low
    )
    spread_inputs = (hot_bf[:, :, None] * inputs_recv[:, None, :]).reshape(
        owners * capacity, DOC_DEV * width_low
    )
    contract = (((0,), (0,)), ((), ()))
    grad_gram = lax.dot_general(
        spread_grads, recv_rows, contract, preferred_element_type=jnp.float32
    ).reshape(DOC_DEV, width_low, 2 * width_low)
    outer_b = grad_gram[:, :, :width_low]
    doc_grad = grad_gram[:, :, width_low:]
    outer_a = lax.dot_general(
        spread_inputs, inputs_recv, contract, preferred_element_type=jnp.float32
    ).reshape(DOC_DEV, width_low, width_low)
    inv_a = inverse_factor(outer_a, counts)
    inv_b = inverse_factor(outer_b, counts)
    tilted = jnp.einsum("dab,dbc->dac", inv_b, doc_grad, precision=HIGHEST_PRECISION)
    tilted = jnp.einsum("dab,dbc->dac", tilted, inv_a, precision=HIGHEST_PRECISION)
    queries = tilted.reshape(DOC_DEV, width_low * width_low).astype(jnp.bfloat16)
    score_dims = (((1,), (1,)), ((), ()))

    def scoring(block):
        return lax.dot_general(
            block, train_rows, score_dims, preferred_element_type=jnp.float32
        ).astype(jnp.bfloat16)

    def step_ahead(current_block, unused):
        arrived = passed_along(current_block, "blk", 1)
        return (arrived, scoring(arrived))

    def step_back(current_block):
        arrived = passed_along(current_block, "blk", -1)
        return (arrived, scoring(arrived))

    def both_ways(carried, unused):
        ahead_block, back_block = carried
        ahead_block, ahead_tile = step_ahead(ahead_block, unused)
        back_block, back_tile = step_back(back_block)
        return ((ahead_block, back_block), (ahead_tile, back_tile))

    last_pair, paired_tiles = lax.scan(both_ways, (queries, queries), None, length=LEAD)
    ahead_tiles, back_tiles = paired_tiles
    tail_block, tail_tiles = lax.scan(step_ahead, last_pair[0], None, length=STOPS - 1 - 2 * LEAD)
    stacked = jnp.concatenate(
        [jnp.flip(back_tiles, 0), scoring(queries)[None], ahead_tiles, tail_tiles], axis=0
    )
    return stacked


def solution(mesh):
    placed = (
        P(("groups", "blk"), None),
        P(("groups", "blk"), None),
        P(),
        P(),
        P(("groups", "blk"), None),
        P(("groups", "blk"), None),
        P(("groups", "blk")),
    )
    return jax.shard_map(
        local,
        mesh=mesh,
        in_specs=placed,
        out_specs=P(None, None, ("groups", "blk")),
        check_vma=False,
    )
```

profile of v0, /device:TPU:0, one launch (start us, length us, event | category | flops | bytes accessed | tf_op | source)
XLA Modules:
  0.0 149.2 jit_solution(2262987183202212464)
XLA Ops:
  2.7 7.4 %all-to-all-start = ((s32[16,1,64]{2,1,0:T(1,128)}), s32[16,1,64]{2,1,0:T(1,128)S(1)}, u32[]{:S(2)}, u32[]{:S(2)}) async-start(s32[16,1,64]{2,1,0:T(1,128)} %all_to_all.9), calls=%async_computation | async-start | bytes 16384 | tf_op jit(solution)/shard_map/all_to_all | solution.py:70
  10.1 1.9 %convolution_convert_fusion.4 = bf16[256,64]{1,0:T(8,128)(2,1)S(1)} fusion(bf16[256,4096]{1,0:T(8,128)(2,1)S(1)} %copy-done, bf16[4096,64]{0,1:T(8,128)(2,1)} %param.11), kind=kOutput, calls=%fused_computation.30 | convolution fusion | flops 134234112 | bytes 2654208 | tf_op jit(solution)/shard_map/dot_general | solution.py:43
  13.8 2.6 %all-to-all-done = s32[16,1,64]{2,1,0:T(1,128)S(1)} async-done(((s32[16,1,64]{2,1,0:T(1,128)}), s32[16,1,64]{2,1,0:T(1,128)S(1)}, u32[]{:S(2)}, u32[]{:S(2)}) %all-to-all-start) | async-done | bytes 4128 | tf_op jit(solution)/shard_map/all_to_all | solution.py:70
  16.4 4.1 %all-to-all-start.1 = ((bf16[16,64,128]{2,1,0:T(8,128)(2,1)}), bf16[16,64,128]{2,1,0:T(8,128)(2,1)S(1)}, u32[]{:S(2)}, u32[]{:S(2)}) async-start(bf16[16,64,128]{2,1,0:T(8,128)(2,1)} %bitcast.3), calls=%async_computation.1 | async-start | bytes 524288 | tf_op jit(solution)/shard_map/all_to_all | solution.py:63
  23.2 6.8 %all-to-all-done.1 = bf16[16,64,128]{2,1,0:T(8,128)(2,1)S(1)} async-done(((bf16[16,64,128]{2,1,0:T(8,128)(2,1)}), bf16[16,64,128]{2,1,0:T(8,128)(2,1)S(1)}, u32[]{:S(2)}, u32[]{:S(2)}) %all-to-all-start.1) | async-done | bytes 262176 | tf_op jit(solution)/shard_map/all_to_all | solution.py:63
  31.6 2.2 %fusion.6 = f32[32,64,128]{2,1,0:T(8,128)S(1)} fusion(bf16[1024,128,1]{1,0,2:T(8,128)(2,1)S(1)} %bitcast.109, bf16[1024,64]{0,1:T(8,128)(2,1)} %copy.12, bf16[1024,32]{0,1:T(8,128)(2,1)} %compare_convert_fusion.1), kind=kOutput, calls=%fused_computation.8 | convolution fusion | flops 538968064 | bytes 1507328 | tf_op jit(solution)/shard_map/dot_general | solution.py:89
  34.8 1.4 reduce_max.18
  36.2 2.1 %convolution_subtract_fusion.11 = f32[32,64,64]{2,1,0:T(8,128)S(1)} fusion(f32[64,64]{1,0:T(8,128)S(1)} %fusion.46, f32[32]{0:T(128)} %reduce_max.18, f32[64,64]{1,0:T(8,128)S(1)} %fusion.47, f32[32,64,128]{2,1,0:T(8,128)S(1)} %fusion.6, f32[32]{0:T(128)} %broadcast_add_fusion.1), kind=kOutput, calls=%fused_computation.27 | convolution fusion | flops 101187584 | bytes 1671424 | tf_op jit(solution)/shard_map/dab,dbc->dac/dot_general | solution.py:28
  38.4 1.2 fusion.29
  39.6 1.3 convolution_subtract_fusion.10
  41.0 1.2 fusion.58
  42.2 1.4 convolution_subtract_fusion.9
  43.5 1.2 fusion.59
  44.8 1.4 convolution_subtract_fusion.8
  46.1 1.4 fusion.60
  47.5 1.4 convolution_subtract_fusion.7
  48.9 1.2 fusion.61
  50.1 1.4 convolution_subtract_fusion.6
  52.6 2.2 %fusion.23 = f32[32,64,64]{2,1,0:T(8,128)} fusion(f32[32,64,64]{2,1,0:T(8,128)S(1)} %fusion.62, f32[32,64,128]{2,1,0:T(8,128)S(1)} %fusion.6), kind=kOutput, calls=%fused_computation.40 | convolution fusion | flops 100663296 | bytes 2097152 | tf_op jit(solution)/shard_map/dab,dbc->dac/dot_general | solution.py:99
  54.8 1.7 %copy.13 = bf16[1024,64]{0,1:T(8,128)(2,1)} copy(bf16[1024,64]{1,0:T(8,128)(2,1)} %get-tuple-element.66) | data formatting | bytes 262144 | tf_op jit(solution)/shard_map/slice | solution.py:81
  56.6 3.0 %abs_reduce_fusion = (f32[32,64]{1,0:T(8,128)}, f32[32,64,64]{2,1,0:T(8,128)S(1)}) fusion(f32[64,64]{1,0:T(8,128)S(1)} %fusion.47, f32[32]{0:T(128)} %broadcast_add_fusion.1, bf16[1024,128]{1,0:T(8,128)(2,1)S(1)} %bitcast.110, bf16[1024,64]{0,1:T(8,128)(2,1)} %copy.13, bf16[1024,32]{0,1:T(8,128)(2,1)} %compare_convert_fusion.1), kind=kOutput, calls=%fused_computation.44 | convolution fusion | flops 271054848 | bytes 1007744 | tf_op jit(solution)/shard_map/dot_general | solution.py:94
  60.4 1.2 convolution_subtract_fusion.5
  61.6 1.2 fusion.26
  62.8 1.2 convolution_subtract_fusion.4
  64.1 1.4 fusion.63
  65.5 1.2 convolution_subtract_fusion.3
  67.9 1.2 convolution_subtract_fusion.2
  70.3 1.2 convolution_subtract_fusion.1
  72.8 1.2 convolution_subtract_fusion
  75.2 1.4 convolution_convert_fusion.2
  77.2 61.7 %while.4 = (s32[]{:T(128)}, bf16[32,4096]{1,0:T(8,128)(2,1)S(1)}, bf16[32,4096]{1,0:T(8,128)(2,1)S(1)}, bf16[5,32,256]{2,1,0:T(8,128)(2,1)}, bf16[5,32,256]{2,1,...) while((s32[]{:T(128)}, bf16[32,4096]{1,0:T(8,128)(2,1)S(1)}, bf16[32,4096]{1,0:T(8,128)(2,1)S(1)}, ...), condition=%wide.region_8.9_spmd, body=%wide.region_7.8_spmd.sunk | while | flops 134234112 | bytes 16285897 | solution.py:123
  77.2 4.4 %collective-permute-start.1 = (bf16[32,4096]{1,0:T(8,128)(2,1)S(1)}, bf16[32,4096]{1,0:T(8,128)(2,1)S(1)}, u32[]{:S(2)}, u32[]{:S(2)}) collective-permute-start(bf16[32,4096]{1,0:T(8,128)(2,1)S(1)} %get-tuple-element.118), channel_id=1, source_target_pairs={{0,15},{1,0},{2,1},{3,2},{4,3},{5,4},{6,5},{7,6},{8,7},{9,8},{10,9... | collective-permute-start | bytes 786440 | tf_op jit(solution)/shard_map/while/body/eval_jaxpr/ppermute | solution.py:18
  81.7 4.2 %collective-permute-done = bf16[32,4096]{1,0:T(8,128)(2,1)S(1)} collective-permute-done((bf16[32,4096]{1,0:T(8,128)(2,1)S(1)}, bf16[32,4096]{1,0:T(8,128)(2,1)S(1)}, u32[]{:S(2)}, u32[]{:S(2)}) %collective-permute-start) | collective-permute-done | bytes 262176 | tf_op jit(solution)/shard_map/while/body/eval_jaxpr/ppermute | solution.py:18
  85.9 2.9 %fusion.132 = bf16[5,32,256]{2,1,0:T(8,128)(2,1)} fusion(bf16[5,32,256]{2,1,0:T(8,128)(2,1)} %get-tuple-element.119, s32[]{:T(128)S(6)} %copy.26, bf16[32,4096]{1,0:T(8,128)(2,1)S(1)} %collective-permute-done, bf16[256,4096]{1,0:T(8,128)(2,1)} %get-tuple-element.128), kind=kOutput, calls=%fused_computation.3.clone.1 | convolution fusion | flops 67117056 | bytes 2375684 | tf_op jit(solution)/shard_map/while/body/eval_jaxpr/dot_general | solution.py:105
  89.6 4.4 %collective-permute-start.1 = (bf16[32,4096]{1,0:T(8,128)(2,1)S(1)}, bf16[32,4096]{1,0:T(8,128)(2,1)S(1)}, u32[]{:S(2)}, u32[]{:S(2)}) collective-permute-start(bf16[32,4096]{1,0:T(8,128)(2,1)S(1)} %get-tuple-element.118), channel_id=1, source_target_pairs={{0,15},{1,0},{2,1},{3,2},{4,3},{5,4},{6,5},{7,6},{8,7},{9,8},{10,9... | collective-permute-start | bytes 786440 | tf_op jit(solution)/shard_map/while/body/eval_jaxpr/ppermute | solution.py:18
  94.0 4.2 %collective-permute-done = bf16[32,4096]{1,0:T(8,128)(2,1)S(1)} collective-permute-done((bf16[32,4096]{1,0:T(8,128)(2,1)S(1)}, bf16[32,4096]{1,0:T(8,128)(2,1)S(1)}, u32[]{:S(2)}, u32[]{:S(2)}) %collective-permute-start) | collective-permute-done | bytes 262176 | tf_op jit(solution)/shard_map/while/body/eval_jaxpr/ppermute | solution.py:18
  98.2 2.9 %fusion.132 = bf16[5,32,256]{2,1,0:T(8,128)(2,1)} fusion(bf16[5,32,256]{2,1,0:T(8,128)(2,1)} %get-tuple-element.119, s32[]{:T(128)S(6)} %copy.26, bf16[32,4096]{1,0:T(8,128)(2,1)S(1)} %collective-permute-done, bf16[256,4096]{1,0:T(8,128)(2,1)} %get-tuple-element.128), kind=kOutput, calls=%fused_computation.3.clone.1 | convolution fusion | flops 67117056 | bytes 2375684 | tf_op jit(solution)/shard_map/while/body/eval_jaxpr/dot_general | solution.py:105
  101.9 4.4 %collective-permute-start.1 = (bf16[32,4096]{1,0:T(8,128)(2,1)S(1)}, bf16[32,4096]{1,0:T(8,128)(2,1)S(1)}, u32[]{:S(2)}, u32[]{:S(2)}) collective-permute-start(bf16[32,4096]{1,0:T(8,128)(2,1)S(1)} %get-tuple-element.118), channel_id=1, source_target_pairs={{0,15},{1,0},{2,1},{3,2},{4,3},{5,4},{6,5},{7,6},{8,7},{9,8},{10,9... | collective-permute-start | bytes 786440 | tf_op jit(solution)/shard_map/while/body/eval_jaxpr/ppermute | solution.py:18
  106.4 4.2 %collective-permute-done = bf16[32,4096]{1,0:T(8,128)(2,1)S(1)} collective-permute-done((bf16[32,4096]{1,0:T(8,128)(2,1)S(1)}, bf16[32,4096]{1,0:T(8,128)(2,1)S(1)}, u32[]{:S(2)}, u32[]{:S(2)}) %collective-permute-start) | collective-permute-done | bytes 262176 | tf_op jit(solution)/shard_map/while/body/eval_jaxpr/ppermute | solution.py:18
  110.6 2.9 %fusion.132 = bf16[5,32,256]{2,1,0:T(8,128)(2,1)} fusion(bf16[5,32,256]{2,1,0:T(8,128)(2,1)} %get-tuple-element.119, s32[]{:T(128)S(6)} %copy.26, bf16[32,4096]{1,0:T(8,128)(2,1)S(1)} %collective-permute-done, bf16[256,4096]{1,0:T(8,128)(2,1)} %get-tuple-element.128), kind=kOutput, calls=%fused_computation.3.clone.1 | convolution fusion | flops 67117056 | bytes 2375684 | tf_op jit(solution)/shard_map/while/body/eval_jaxpr/dot_general | solution.py:105
  114.3 4.4 %collective-permute-start.1 = (bf16[32,4096]{1,0:T(8,128)(2,1)S(1)}, bf16[32,4096]{1,0:T(8,128)(2,1)S(1)}, u32[]{:S(2)}, u32[]{:S(2)}) collective-permute-start(bf16[32,4096]{1,0:T(8,128)(2,1)S(1)} %get-tuple-element.118), channel_id=1, source_target_pairs={{0,15},{1,0},{2,1},{3,2},{4,3},{5,4},{6,5},{7,6},{8,7},{9,8},{10,9... | collective-permute-start | bytes 786440 | tf_op jit(solution)/shard_map/while/body/eval_jaxpr/ppermute | solution.py:18
  118.7 4.2 %collective-permute-done = bf16[32,4096]{1,0:T(8,128)(2,1)S(1)} collective-permute-done((bf16[32,4096]{1,0:T(8,128)(2,1)S(1)}, bf16[32,4096]{1,0:T(8,128)(2,1)S(1)}, u32[]{:S(2)}, u32[]{:S(2)}) %collective-permute-start) | collective-permute-done | bytes 262176 | tf_op jit(solution)/shard_map/while/body/eval_jaxpr/ppermute | solution.py:18
  122.9 2.9 %fusion.132 = bf16[5,32,256]{2,1,0:T(8,128)(2,1)} fusion(bf16[5,32,256]{2,1,0:T(8,128)(2,1)} %get-tuple-element.119, s32[]{:T(128)S(6)} %copy.26, bf16[32,4096]{1,0:T(8,128)(2,1)S(1)} %collective-permute-done, bf16[256,4096]{1,0:T(8,128)(2,1)} %get-tuple-element.128), kind=kOutput, calls=%fused_computation.3.clone.1 | convolution fusion | flops 67117056 | bytes 2375684 | tf_op jit(solution)/shard_map/while/body/eval_jaxpr/dot_general | solution.py:105
  126.7 4.4 %collective-permute-start.1 = (bf16[32,4096]{1,0:T(8,128)(2,1)S(1)}, bf16[32,4096]{1,0:T(8,128)(2,1)S(1)}, u32[]{:S(2)}, u32[]{:S(2)}) collective-permute-start(bf16[32,4096]{1,0:T(8,128)(2,1)S(1)} %get-tuple-element.118), channel_id=1, source_target_pairs={{0,15},{1,0},{2,1},{3,2},{4,3},{5,4},{6,5},{7,6},{8,7},{9,8},{10,9... | collective-permute-start | bytes 786440 | tf_op jit(solution)/shard_map/while/body/eval_jaxpr/ppermute | solution.py:18
  131.0 4.2 %collective-permute-done = bf16[32,4096]{1,0:T(8,128)(2,1)S(1)} collective-permute-done((bf16[32,4096]{1,0:T(8,128)(2,1)S(1)}, bf16[32,4096]{1,0:T(8,128)(2,1)S(1)}, u32[]{:S(2)}, u32[]{:S(2)}) %collective-permute-start) | collective-permute-done | bytes 262176 | tf_op jit(solution)/shard_map/while/body/eval_jaxpr/ppermute | solution.py:18
  135.2 2.9 %fusion.132 = bf16[5,32,256]{2,1,0:T(8,128)(2,1)} fusion(bf16[5,32,256]{2,1,0:T(8,128)(2,1)} %get-tuple-element.119, s32[]{:T(128)S(6)} %copy.26, bf16[32,4096]{1,0:T(8,128)(2,1)S(1)} %collective-permute-done, bf16[256,4096]{1,0:T(8,128)(2,1)} %get-tuple-element.128), kind=kOutput, calls=%fused_computation.3.clone.1 | convolution fusion | flops 67117056 | bytes 2375684 | tf_op jit(solution)/shard_map/while/body/eval_jaxpr/dot_general | solution.py:105
  139.1 2.5 %fusion.20 = bf16[1,32,256]{2,1,0:T(8,128)(2,1)S(1)} fusion(bf16[32,4096]{1,0:T(8,128)(2,1)S(1)} %convert_element_type.71, bf16[256,4096]{1,0:T(8,128)(2,1)} %get-tuple-element.130), kind=kOutput, calls=%fused_computation.37 | convolution fusion | flops 67117056 | bytes 2375680 | tf_op jit(solution)/shard_map/dot_general | solution.py:105
  141.6 5.9 %collective-permute-done.2 = bf16[32,4096]{1,0:T(8,128)(2,1)S(1)} collective-permute-done((bf16[32,4096]{1,0:T(8,128)(2,1)S(1)}, bf16[32,4096]{1,0:T(8,128)(2,1)S(1)}, u32[]{:S(2)}, u32[]{:S(2)}) %collective-permute-start.2) | collective-permute-done | bytes 262176 | tf_op jit(solution)/shard_map/while/body/eval_jaxpr/ppermute | solution.py:18
  (86 shorter events, 22.9 us)
Async XLA Ops:
  0.0 10.1 %copy-start = (bf16[256,4096]{1,0:T(8,128)(2,1)S(1)}, bf16[256,4096]{1,0:T(8,128)(2,1)}, u32[]{:S(2)}) copy-start(bf16[256,4096]{1,0:T(8,128)(2,1)} %param.9) | copy-start | bytes 6291460
  0.0 12.0 %copy-start.9 = (bf16[4096,64]{0,1:T(8,128)(2,1)S(1)}, bf16[4096,64]{0,1:T(8,128)(2,1)}, u32[]{:S(2)}) copy-start(bf16[4096,64]{0,1:T(8,128)(2,1)} %param.12) | copy-start | bytes 1572868
  2.7 13.8 %all-to-all-start = ((s32[16,1,64]{2,1,0:T(1,128)}), s32[16,1,64]{2,1,0:T(1,128)S(1)}, u32[]{:S(2)}, u32[]{:S(2)}) async-start(s32[16,1,64]{2,1,0:T(1,128)} %all_to_all.9), calls=%async_computation | async-start | bytes 16384 | tf_op jit(solution)/shard_map/all_to_all | solution.py:70
  10.1 1.9 %copy-start.8 = (bf16[256,4096]{1,0:T(8,128)(2,1)S(1)}, bf16[256,4096]{1,0:T(8,128)(2,1)}, u32[]{:S(2)}) copy-start(bf16[256,4096]{1,0:T(8,128)(2,1)} %param.10) | copy-start | bytes 6291460
  16.4 13.5 %all-to-all-start.1 = ((bf16[16,64,128]{2,1,0:T(8,128)(2,1)}), bf16[16,64,128]{2,1,0:T(8,128)(2,1)S(1)}, u32[]{:S(2)}, u32[]{:S(2)}) async-start(bf16[16,64,128]{2,1,0:T(8,128)(2,1)} %bitcast.3), calls=%async_computation.1 | async-start | bytes 524288 | tf_op jit(solution)/shard_map/all_to_all | solution.py:63
  31.6 2.2 %copy-start.5 = (f32[32]{0:T(128)S(1)}, f32[32]{0:T(128)}, u32[]{:S(2)}) copy-start(f32[32]{0:T(128)} %broadcast_add_fusion.1) | copy-start | bytes 388
  36.2 2.1 %copy-start.7 = (f32[32]{0:T(128)S(1)}, f32[32]{0:T(128)}, u32[]{:S(2)}) copy-start(f32[32]{0:T(128)} %reduce_max.18) | copy-start | bytes 388
  38.3 1.3 copy-start.6
  74.0 1.2 copy-start.3
  77.2 8.6 %collective-permute-start = (bf16[32,4096]{1,0:T(8,128)(2,1)S(1)}, bf16[32,4096]{1,0:T(8,128)(2,1)S(1)}, u32[]{:S(2)}, u32[]{:S(2)}) collective-permute-start(bf16[32,4096]{1,0:T(8,128)(2,1)S(1)} %get-tuple-element.117), channel_id=1, source_target_pairs={{0,1},{1,2},{2,3},{3,4},{4,5},{5,6},{6,7},{7,8},{8,9},{9,10},{10,1... | collective-permute-start | bytes 786440 | tf_op jit(solution)/shard_map/while/body/eval_jaxpr/ppermute | solution.py:18
  77.2 8.6 %collective-permute-start.1 = (bf16[32,4096]{1,0:T(8,128)(2,1)S(1)}, bf16[32,4096]{1,0:T(8,128)(2,1)S(1)}, u32[]{:S(2)}, u32[]{:S(2)}) collective-permute-start(bf16[32,4096]{1,0:T(8,128)(2,1)S(1)} %get-tuple-element.118), channel_id=1, source_target_pairs={{0,15},{1,0},{2,1},{3,2},{4,3},{5,4},{6,5},{7,6},{8,7},{9,8},{10,9... | collective-permute-start | bytes 786440 | tf_op jit(solution)/shard_map/while/body/eval_jaxpr/ppermute | solution.py:18
  81.7 7.1 %copy-start.1 = (bf16[256,4096]{1,0:T(8,128)(2,1)S(1)}, bf16[256,4096]{1,0:T(8,128)(2,1)}, u32[]{:S(2)}) copy-start(bf16[256,4096]{1,0:T(8,128)(2,1)} %get-tuple-element.128) | copy-start | bytes 6291460 | tf_op jit(solution)/shard_map/while
  89.6 8.6 %collective-permute-start = (bf16[32,4096]{1,0:T(8,128)(2,1)S(1)}, bf16[32,4096]{1,0:T(8,128)(2,1)S(1)}, u32[]{:S(2)}, u32[]{:S(2)}) collective-permute-start(bf16[32,4096]{1,0:T(8,128)(2,1)S(1)} %get-tuple-element.117), channel_id=1, source_target_pairs={{0,1},{1,2},{2,3},{3,4},{4,5},{5,6},{6,7},{7,8},{8,9},{9,10},{10,1... | collective-permute-start | bytes 786440 | tf_op jit(solution)/shard_map/while/body/eval_jaxpr/ppermute | solution.py:18
  89.6 8.6 %collective-permute-start.1 = (bf16[32,4096]{1,0:T(8,128)(2,1)S(1)}, bf16[32,4096]{1,0:T(8,128)(2,1)S(1)}, u32[]{:S(2)}, u32[]{:S(2)}) collective-permute-start(bf16[32,4096]{1,0:T(8,128)(2,1)S(1)} %get-tuple-element.118), channel_id=1, source_target_pairs={{0,15},{1,0},{2,1},{3,2},{4,3},{5,4},{6,5},{7,6},{8,7},{9,8},{10,9... | collective-permute-start | bytes 786440 | tf_op jit(solution)/shard_map/while/body/eval_jaxpr/ppermute | solution.py:18
  94.0 7.2 %copy-start.1 = (bf16[256,4096]{1,0:T(8,128)(2,1)S(1)}, bf16[256,4096]{1,0:T(8,128)(2,1)}, u32[]{:S(2)}) copy-start(bf16[256,4096]{1,0:T(8,128)(2,1)} %get-tuple-element.128) | copy-start | bytes 6291460 | tf_op jit(solution)/shard_map/while
  101.9 8.6 %collective-permute-start = (bf16[32,4096]{1,0:T(8,128)(2,1)S(1)}, bf16[32,4096]{1,0:T(8,128)(2,1)S(1)}, u32[]{:S(2)}, u32[]{:S(2)}) collective-permute-start(bf16[32,4096]{1,0:T(8,128)(2,1)S(1)} %get-tuple-element.117), channel_id=1, source_target_pairs={{0,1},{1,2},{2,3},{3,4},{4,5},{5,6},{6,7},{7,8},{8,9},{9,10},{10,1... | collective-permute-start | bytes 786440 | tf_op jit(solution)/shard_map/while/body/eval_jaxpr/ppermute | solution.py:18
  101.9 8.6 %collective-permute-start.1 = (bf16[32,4096]{1,0:T(8,128)(2,1)S(1)}, bf16[32,4096]{1,0:T(8,128)(2,1)S(1)}, u32[]{:S(2)}, u32[]{:S(2)}) collective-permute-start(bf16[32,4096]{1,0:T(8,128)(2,1)S(1)} %get-tuple-element.118), channel_id=1, source_target_pairs={{0,15},{1,0},{2,1},{3,2},{4,3},{5,4},{6,5},{7,6},{8,7},{9,8},{10,9... | collective-permute-start | bytes 786440 | tf_op jit(solution)/shard_map/while/body/eval_jaxpr/ppermute | solution.py:18
  106.4 7.2 %copy-start.1 = (bf16[256,4096]{1,0:T(8,128)(2,1)S(1)}, bf16[256,4096]{1,0:T(8,128)(2,1)}, u32[]{:S(2)}) copy-start(bf16[256,4096]{1,0:T(8,128)(2,1)} %get-tuple-element.128) | copy-start | bytes 6291460 | tf_op jit(solution)/shard_map/while
  114.2 8.6 %collective-permute-start = (bf16[32,4096]{1,0:T(8,128)(2,1)S(1)}, bf16[32,4096]{1,0:T(8,128)(2,1)S(1)}, u32[]{:S(2)}, u32[]{:S(2)}) collective-permute-start(bf16[32,4096]{1,0:T(8,128)(2,1)S(1)} %get-tuple-element.117), channel_id=1, source_target_pairs={{0,1},{1,2},{2,3},{3,4},{4,5},{5,6},{6,7},{7,8},{8,9},{9,10},{10,1... | collective-permute-start | bytes 786440 | tf_op jit(solution)/shard_map/while/body/eval_jaxpr/ppermute | solution.py:18
  114.3 8.6 %collective-permute-start.1 = (bf16[32,4096]{1,0:T(8,128)(2,1)S(1)}, bf16[32,4096]{1,0:T(8,128)(2,1)S(1)}, u32[]{:S(2)}, u32[]{:S(2)}) collective-permute-start(bf16[32,4096]{1,0:T(8,128)(2,1)S(1)} %get-tuple-element.118), channel_id=1, source_target_pairs={{0,15},{1,0},{2,1},{3,2},{4,3},{5,4},{6,5},{7,6},{8,7},{9,8},{10,9... | collective-permute-start | bytes 786440 | tf_op jit(solution)/shard_map/while/body/eval_jaxpr/ppermute | solution.py:18
  118.7 7.2 %copy-start.1 = (bf16[256,4096]{1,0:T(8,128)(2,1)S(1)}, bf16[256,4096]{1,0:T(8,128)(2,1)}, u32[]{:S(2)}) copy-start(bf16[256,4096]{1,0:T(8,128)(2,1)} %get-tuple-element.128) | copy-start | bytes 6291460 | tf_op jit(solution)/shard_map/while
  126.6 8.6 %collective-permute-start = (bf16[32,4096]{1,0:T(8,128)(2,1)S(1)}, bf16[32,4096]{1,0:T(8,128)(2,1)S(1)}, u32[]{:S(2)}, u32[]{:S(2)}) collective-permute-start(bf16[32,4096]{1,0:T(8,128)(2,1)S(1)} %get-tuple-element.117), channel_id=1, source_target_pairs={{0,1},{1,2},{2,3},{3,4},{4,5},{5,6},{6,7},{7,8},{8,9},{9,10},{10,1... | collective-permute-start | bytes 786440 | tf_op jit(solution)/shard_map/while/body/eval_jaxpr/ppermute | solution.py:18
  126.7 8.5 %collective-permute-start.1 = (bf16[32,4096]{1,0:T(8,128)(2,1)S(1)}, bf16[32,4096]{1,0:T(8,128)(2,1)S(1)}, u32[]{:S(2)}, u32[]{:S(2)}) collective-permute-start(bf16[32,4096]{1,0:T(8,128)(2,1)S(1)} %get-tuple-element.118), channel_id=1, source_target_pairs={{0,15},{1,0},{2,1},{3,2},{4,3},{5,4},{6,5},{7,6},{8,7},{9,8},{10,9... | collective-permute-start | bytes 786440 | tf_op jit(solution)/shard_map/while/body/eval_jaxpr/ppermute | solution.py:18
  131.0 7.2 %copy-start.1 = (bf16[256,4096]{1,0:T(8,128)(2,1)S(1)}, bf16[256,4096]{1,0:T(8,128)(2,1)}, u32[]{:S(2)}) copy-start(bf16[256,4096]{1,0:T(8,128)(2,1)} %get-tuple-element.128) | copy-start | bytes 6291460 | tf_op jit(solution)/shard_map/while
  138.9 8.5 %collective-permute-start.2 = (bf16[32,4096]{1,0:T(8,128)(2,1)S(1)}, bf16[32,4096]{1,0:T(8,128)(2,1)S(1)}, u32[]{:S(2)}, u32[]{:S(2)}) collective-permute-start(bf16[32,4096]{1,0:T(8,128)(2,1)S(1)} %get-tuple-element.53), channel_id=1, source_target_pairs={{0,1},{1,2},{2,3},{3,4},{4,5},{5,6},{6,7},{7,8},{8,9},{9,10},{10,1... | collective-permute-start | bytes 786440 | tf_op jit(solution)/shard_map/while/body/eval_jaxpr/ppermute | solution.py:18
  139.1 8.4 %copy-start.2 = (bf16[256,4096]{1,0:T(8,128)(2,1)S(1)}, bf16[256,4096]{1,0:T(8,128)(2,1)}, u32[]{:S(2)}) copy-start(bf16[256,4096]{1,0:T(8,128)(2,1)} %get-tuple-element.130) | copy-start | bytes 6291460
  139.1 9.1 %copy-start.4 = (bf16[5,32,256]{2,1,0:T(8,128)(2,1)S(1)}, bf16[5,32,256]{2,1,0:T(8,128)(2,1)}, u32[]{:S(2)}) copy-start(bf16[5,32,256]{2,1,0:T(8,128)(2,1)} %get-tuple-element.52) | copy-start | bytes 245764
where the time goes:
time: 152 us; the launch traced here: 149 us
  matrix products  66 us (43%)
  waiting for transfers between devices  36 us (24%)
  starting transfers between devices  34 us (22%)
  other arithmetic  7.02 us (5%)
  local copies, waits for them, and re-layouts  5.39 us (4%)
    ppermute x11, waiting for transfers between devices, passed_along(): return lax.ppermute(value, axis, pairs)  26.6 us
    ppermute x11, starting transfers between devices, passed_along(): return lax.ppermute(value, axis, pairs)  22.5 us
    dot_general x12, matrix products, scoring(): lax.dot_general(block, train_rows, score_dims, preferred_element_type=jnp...  21.5 us
    dot_general x12, matrix products, inverse_factor(): jnp.einsum('dab,dbc->dac', damped, approx, precision=HIGHEST_PRECISION)  16.1 us
    dot_general x12, matrix products, inverse_factor(): jnp.einsum('dab,dbc->dac', approx, 2.0 * identity_mat[None] - product, pr...  14.9 us
    all_to_all x1, starting transfers between devices, local(): lax.all_to_all(send_slot.reshape(owners, capacity), 'blk', split_axis=0,...  7.41 us
    all_to_all x1, waiting for transfers between devices, local(): lax.all_to_all(send_rows.reshape(owners, capacity, 2 * width_low), 'blk',...  6.77 us
    all_to_all x1, starting transfers between devices, local(): lax.all_to_all(send_rows.reshape(owners, capacity, 2 * width_low), 'blk',...  4.06 us
  transfers between devices with their start and end apart: 13, of which 8 were waited for; matrix products, arithmetic and copies ran while one was open for 6% of the time, Pallas kernels for 0%

commit v1 on v0

v1 whole, which is shorter than its diff:
```python
import functools

import jax
import jax.numpy as jnp
from jax import lax
from jax.experimental import pallas as pl
from jax.experimental.pallas import tpu as pltpu
from jax.sharding import PartitionSpec as P

DOC_DEV = 32
STOPS = 12
NEWTON_STEPS = 6
LEAD = 5
LANES = 128
DOC_GROUP = 4
MESH = pl.DeviceIdType.MESH
VMEM_SPEC = pl.BlockSpec(memory_space=pltpu.VMEM)
F32 = jnp.float32
BF16 = jnp.bfloat16
CONTRACT_LAST = (((1,), (1,)), ((), ()))


def matmul(left, right):
    return jnp.dot(left, right, preferred_element_type=F32)


def halves(value):
    high = value.astype(BF16)
    return high, (value - high.astype(F32)).astype(BF16)


def split_matmul(left, right):
    left_high, left_low = left
    right_high, right_low = right
    joined = matmul(
        jnp.concatenate([left_high, left_low], axis=1),
        jnp.concatenate([right_high, right_high], axis=0),
    )
    return joined + matmul(left_high, right_low)


def dispatch_kernel(owners, capacity, x_in, x_grad, p_in, p_out, owner_col, owner_row, slot_row,
                    recv_rows, recv_slot, low, send_rows, send_slot,
                    rows_sent, rows_here, slot_sent, slot_here):
    me = lax.axis_index("blk")
    barrier = pltpu.get_barrier_semaphore()

    @pl.loop(1, owners)
    def _(ahead):
        pl.semaphore_signal(
            barrier, inc=1, device_id={"blk": lax.rem(me + ahead, owners)}, device_id_type=MESH
        )

    count = x_in.shape[0]
    width = p_in.shape[1]
    low[:, :width] = matmul(x_grad[...], p_out[...]).astype(BF16)
    low[:, width:] = matmul(x_in[...], p_in[...]).astype(BF16)
    token = lax.broadcasted_iota(jnp.int32, (count, count), 0)
    other = lax.broadcasted_iota(jnp.int32, (count, count), 1)
    same = (owner_col[...] == owner_row[...]) & (token < other)
    rank = jnp.sum(jnp.where(same, 1.0, 0.0), axis=0, keepdims=True).astype(jnp.int32)
    position = owner_row[...] * capacity + rank
    place = lax.broadcasted_iota(jnp.int32, (owners * capacity, count), 0)
    placed = jnp.where(place == position, 1.0, 0.0).astype(BF16)
    send_rows[...] = matmul(placed, low[...]).astype(BF16).reshape(send_rows.shape)
    owner_id = lax.broadcasted_iota(jnp.int32, (owners, count), 0)
    coded = jnp.where(owner_id == owner_row[...], slot_row[...] + 1, 0).astype(F32).astype(BF16)
    lane = lax.broadcasted_iota(jnp.int32, (LANES, count), 0)
    shift = lax.rem(me, LANES // capacity) * capacity
    spread = jnp.where(lane == rank + shift, 1.0, 0.0).astype(BF16)
    codes = lax.dot_general(coded, spread, CONTRACT_LAST, preferred_element_type=F32)
    codes = codes.astype(jnp.int32)
    for owner in range(owners):
        send_slot[owner] = codes[owner:owner + 1]
    pl.semaphore_wait(barrier, owners - 1)

    def copies(target, source, sem):
        to = {"blk": target}
        return (
            pltpu.make_async_remote_copy(
                src_ref=send_rows.at[target], dst_ref=recv_rows.at[source],
                send_sem=rows_sent.at[target], recv_sem=rows_here.at[sem],
                device_id=to, device_id_type=MESH),
            pltpu.make_async_remote_copy(
                src_ref=send_slot.at[target], dst_ref=recv_slot.at[source],
                send_sem=slot_sent.at[target], recv_sem=slot_here.at[sem],
                device_id=to, device_id_type=MESH),
        )

    @pl.loop(1, owners)
    def _(ahead):
        for copy in copies(lax.rem(me + ahead, owners), me, me):
            copy.start()

    recv_rows[me] = send_rows[me]
    recv_slot[me] = send_slot[me]

    @pl.loop(1, owners)
    def _(ahead):
        source = lax.rem(me + ahead, owners)
        for copy in copies(source, source, source):
            copy.wait_recv()

    @pl.loop(1, owners)
    def _(ahead):
        for copy in copies(lax.rem(me + ahead, owners), me, me):
            copy.wait_send()


def dispatch(x_in, x_grad, p_in, p_out, owner_col, owner_row, slot_row):
    owners = lax.axis_size("blk")
    count, width = x_in.shape[0], p_in.shape[1]
    capacity = 4 * count // owners
    rows = (owners, capacity, 2 * width)
    slots = (owners, 1, LANES)
    return pl.pallas_call(
        functools.partial(dispatch_kernel, owners, capacity),
        out_shape=(jax.ShapeDtypeStruct(rows, BF16), jax.ShapeDtypeStruct(slots, jnp.int32)),
        in_specs=[VMEM_SPEC] * 7,
        out_specs=(VMEM_SPEC, VMEM_SPEC),
        scratch_shapes=[
            pltpu.VMEM((count, 2 * width), BF16),
            pltpu.VMEM(rows, BF16),
            pltpu.VMEM(slots, jnp.int32),
        ] + [pltpu.SemaphoreType.DMA((owners,))] * 4,
        compiler_params=pltpu.CompilerParams(collective_id=0, has_side_effects=True),
        name="dispatch",
    )(x_in, x_grad, p_in, p_out, owner_col, owner_row, slot_row)


def queries_kernel(recv_rows, recv_slot, out, turned, codes, flat):
    owners, capacity, full = recv_rows.shape
    width = full // 2
    total = owners * capacity
    group = LANES // capacity
    rows = recv_rows[...].reshape(total, full)
    for part in range(total // LANES):
        span = slice(part * LANES, (part + 1) * LANES)
        turned[:, span] = rows[span].T
        code = recv_slot[part * group]
        for source in range(part * group + 1, (part + 1) * group):
            code = code + recv_slot[source]
        codes[:, span] = code
    row = lax.broadcasted_iota(jnp.int32, (full, full), 0)
    col = lax.broadcasted_iota(jnp.int32, (full, full), 1)
    upper_row = row < width
    diagonal = upper_row == (col < width)
    corner = upper_row & (col >= width)
    identity_mat = jnp.where(row == col, 1.0, 0.0)
    upper = lax.broadcasted_iota(jnp.int32, (full, 1), 0) < width

    @pl.loop(0, DOC_DEV // DOC_GROUP)
    def _(step):
        docs = range(DOC_GROUP)
        code = codes[...]
        counts, masked = [], []
        for doc in docs:
            hot = jnp.where(code == step * DOC_GROUP + doc + 1, 1.0, 0.0)
            counts.append(jnp.sum(hot, axis=1, keepdims=True))
            masked.append(turned[...] * hot.astype(BF16))
        grams = matmul(jnp.concatenate(masked, axis=0), rows)
        grams = [grams[doc * full:(doc + 1) * full] for doc in docs]
        powers, approx = [], []
        for doc in docs:
            damped = jnp.where(diagonal, grams[doc] / (counts[doc] + 1.0), 0.0) + identity_mat
            sums = jnp.sum(jnp.abs(damped), axis=1, keepdims=True)
            bound = jnp.where(
                upper,
                jnp.max(sums[:width], axis=0, keepdims=True),
                jnp.max(sums[width:], axis=0, keepdims=True),
            )
            scale = 1.0 / bound
            residual = identity_mat - damped * scale
            approx.append((identity_mat + residual) * scale)
            parts = halves(residual)
            powers.append(split_matmul(parts, parts))
        for level in range(NEWTON_STEPS - 2):
            for doc in docs:
                power = halves(powers[doc])
                inverse = halves(approx[doc])
                both = tuple(
                    jnp.concatenate([p, x], axis=1) for p, x in zip(power, inverse)
                )
                product = split_matmul(power, both)
                powers[doc] = product[:, :full]
                approx[doc] = approx[doc] + product[:, full:]
        for doc in docs:
            inverse = approx[doc] + split_matmul(halves(powers[doc]), halves(approx[doc]))
            mixed = jnp.where(corner, grams[doc], 0.0)
            tilted = split_matmul(halves(inverse[:width]), halves(mixed))
            right = inverse[width:]
            right = right + pltpu.roll(right, width, 1)
            right = jnp.concatenate([jnp.zeros_like(right), right], axis=0)
            tilted = split_matmul(halves(tilted), halves(right))
            start = pl.multiple_of((step * DOC_GROUP + doc) * width, width)
            flat[pl.ds(start, width), :] = tilted

    left = lax.broadcasted_iota(jnp.int32, (DOC_DEV, full), 1) < width
    for pair in range(width // 2):
        even = flat[pl.ds(2 * pair, DOC_DEV, stride=width), :]
        odd = flat[pl.ds(2 * pair + 1, DOC_DEV, stride=width), :]
        out[:, pair * full:(pair + 1) * full] = jnp.where(left, even, odd).astype(BF16)


def make_queries(recv_rows, recv_slot):
    owners, capacity, full = recv_rows.shape
    width = full // 2
    total = owners * capacity
    return pl.pallas_call(
        queries_kernel,
        out_shape=jax.ShapeDtypeStruct((DOC_DEV, width * width), BF16),
        in_specs=[VMEM_SPEC] * 2,
        out_specs=VMEM_SPEC,
        scratch_shapes=[
            pltpu.VMEM((full, total), BF16),
            pltpu.VMEM((1, total), jnp.int32),
            pltpu.VMEM((DOC_DEV * width, full), F32),
        ],
        name="queries",
    )(recv_rows, recv_slot)


def score_into(out, index, block, train):
    out[index] = lax.dot_general(
        block[...], train[...], CONTRACT_LAST, preferred_element_type=F32
    ).astype(BF16)


def window_kernel(owners, queries, train, out, held, sent, here):
    me = lax.axis_index("blk")
    barrier = pltpu.get_barrier_semaphore()

    def peer(stop):
        return lax.rem(me + stop - LEAD + owners, owners)

    def source(stop):
        return lax.rem(me - stop + LEAD + owners, owners)

    def copy(stop):
        return pltpu.make_async_remote_copy(
            src_ref=queries, dst_ref=held.at[stop], send_sem=sent.at[stop],
            recv_sem=here.at[stop], device_id={"blk": peer(stop)}, device_id_type=MESH)

    others = [stop for stop in range(STOPS) if stop != LEAD]
    for stop in others:
        pl.semaphore_signal(
            barrier, inc=1, device_id={"blk": source(stop)}, device_id_type=MESH
        )
    pl.semaphore_wait(barrier, len(others))
    for stop in others:
        copy(stop).start()
    score_into(out, LEAD, queries, train)
    for stop in others:
        copy(stop).wait_recv()
        score_into(out, stop, held.at[stop], train)
    for stop in others:
        copy(stop).wait_send()


def grid_kernel(owners, queries, train, out, held, up_sent, down_sent, side_sent, twin_sent, here):
    lines = owners // 4
    me = lax.axis_index("blk")
    core = lax.rem(me, 2)
    side = lax.rem(me // 2, 2)
    line = me // 4
    twin = me + 1 - 2 * core
    across = me + 2 - 4 * side
    across_twin = across + 1 - 2 * core
    has_up, has_down = line + 1 < lines, line > 0

    def stop_of(device, origin):
        return lax.rem(device - origin + LEAD + owners, owners)

    def wants(device, origin):
        return stop_of(device, origin) < STOPS

    def copy(source, origin, sems, device):
        return pltpu.make_async_remote_copy(
            src_ref=source, dst_ref=held.at[origin], send_sem=sems.at[origin],
            recv_sem=here.at[origin], device_id={"blk": device}, device_id_type=MESH)

    barrier = pltpu.get_barrier_semaphore()

    def greet(device):
        pl.semaphore_signal(barrier, inc=1, device_id={"blk": device}, device_id_type=MESH)

    greet(twin)
    greet(across)
    pl.when(has_up)(lambda: greet(me + 4))
    pl.when(has_down)(lambda: greet(me - 4))
    pl.semaphore_wait(barrier, 2 + has_up.astype(jnp.int32) + has_down.astype(jnp.int32))

    pl.when(has_up)(lambda: copy(queries, me, up_sent, me + 4).start())
    pl.when(has_down)(lambda: copy(queries, me, down_sent, me - 4).start())
    copy(queries, me, side_sent, across).start()
    copy(queries, me, twin_sent, twin).start()
    held[me] = queries[...]

    def candidate(stage, index):
        way, column, plane = lax.rem(index, 2), lax.rem(index // 2, 2), index // 4
        distance = stage - column
        spot = line + distance * (2 * way - 1)
        near = lax.rem(side + column, 2)
        origin = (spot * 2 + near) * 2 + lax.rem(core + plane, 2)
        real = (spot >= 0) & (spot < lines) & (distance >= 0)
        real = real & ((distance > 0) | (way == 0))
        return way, column, plane, origin, real

    def passes(stage, index, act):
        way, column, _, origin, real = candidate(stage, index)
        straight = real & (column == 0)
        pl.when(straight & (way == 0) & has_up)(
            lambda: act(copy(held.at[origin], origin, up_sent, me + 4)))
        pl.when(straight & (way == 1) & has_down)(
            lambda: act(copy(held.at[origin], origin, down_sent, me - 4)))
        pl.when(straight & (wants(across, origin) | wants(across_twin, origin)))(
            lambda: act(copy(held.at[origin], origin, side_sent, across)))
        pl.when(real & ((column == 0) | wants(me, origin) | wants(twin, origin)) & wants(twin, origin))(
            lambda: act(copy(held.at[origin], origin, twin_sent, twin)))

    @pl.loop(0, lines + 1)
    def _(stage):
        @pl.when(stage > 0)
        def _():
            @pl.loop(0, 4)
            def _(index):
                _, column, _, origin, real = candidate(stage, index)
                comes = real & ((column == 0) | wants(me, origin) | wants(twin, origin))

                @pl.when(comes)
                def _():
                    copy(held.at[origin], origin, twin_sent, twin).wait_recv()

                passes(stage, index, lambda c: c.start())

        @pl.loop(0, 8)
        def _(index):
            _, _, plane, origin, real = candidate(stage, index)

            @pl.when(real & wants(me, origin))
            def _():
                @pl.when(plane == 1)
                def _():
                    copy(held.at[origin], origin, twin_sent, twin).wait_recv()

                score_into(out, stop_of(me, origin), held.at[origin], train)

    pl.when(has_up)(lambda: copy(queries, me, up_sent, me + 4).wait_send())
    pl.when(has_down)(lambda: copy(queries, me, down_sent, me - 4).wait_send())
    copy(queries, me, side_sent, across).wait_send()
    copy(queries, me, twin_sent, twin).wait_send()

    @pl.loop(1, lines + 1)
    def _(stage):
        @pl.loop(0, 4)
        def _(index):
            passes(stage, index, lambda c: c.wait_send())


def influence_of(queries, train):
    owners = lax.axis_size("blk")
    whole_grid = owners % 4 == 0 and owners < 2 * STOPS
    held = owners if whole_grid else STOPS
    kernel = grid_kernel if whole_grid else window_kernel
    return pl.pallas_call(
        functools.partial(kernel, owners),
        out_shape=jax.ShapeDtypeStruct((STOPS, DOC_DEV, train.shape[0]), BF16),
        in_specs=[VMEM_SPEC] * 2,
        out_specs=VMEM_SPEC,
        scratch_shapes=[pltpu.VMEM((held,) + queries.shape, BF16)]
        + [pltpu.SemaphoreType.DMA((held,))] * (5 if whole_grid else 2),
        compiler_params=pltpu.CompilerParams(collective_id=1, has_side_effects=True),
        name="influence",
    )(queries, train)


def local(query_inputs, query_grads, proj_in, proj_out, train_rows, token_owner, token_slot):
    recv_rows, recv_slot = dispatch(
        query_inputs, query_grads, proj_in, proj_out,
        token_owner, token_owner.reshape(1, -1), token_slot.reshape(1, -1),
    )
    return influence_of(make_queries(recv_rows, recv_slot), train_rows)


def solution(mesh):
    placed = (
        P(("groups", "blk"), None),
        P(("groups", "blk"), None),
        P(),
        P(),
        P(("groups", "blk"), None),
        P(("groups", "blk"), None),
        P(("groups", "blk")),
    )
    return jax.shard_map(
        local,
        mesh=mesh,
        in_specs=placed,
        out_specs=P(None, None, ("groups", "blk")),
        check_vma=False,
    )
```

time: 152 us -> 87.4 us (0.58); the launches traced: 149 us -> 86.8 us
  Pallas kernels: 0 us -> 78.9 us
  matrix products: 66 us -> 0 us
  waiting for transfers between devices: 36 us -> 0 us
  starting transfers between devices: 34 us -> 0 us
  other arithmetic: 7.02 us -> 0 us
  local copies, waits for them, and re-layouts: 5.39 us -> 7.88 us
    pallas_call x0 -> x3, Pallas kernels: none -> 78.9 us  [the longest x1 37 us: influence_of(): pl.pallas_call(functools.partial(kernel, owners), out_shape=jax.ShapeDtyp...]
    dot_general x44 -> x0, matrix products: 66 us -> none  [the longest x12 21.5 us: scoring(): lax.dot_general(block, train_rows, score_dims, preferred_element_type=jnp...]
    ppermute x11 -> x0, waiting for transfers between devices: 26.6 us -> none  [passed_along(): return lax.ppermute(value, axis, pairs)]
    ppermute x11 -> x0, starting transfers between devices: 22.5 us -> none  [passed_along(): return lax.ppermute(value, axis, pairs)]
    all_to_all x2 -> x0, starting transfers between devices: 11.5 us -> none  [the longest x1 7.41 us: local(): lax.all_to_all(send_slot.reshape(owners, capacity), 'blk', split_axis=0,...]
    all_to_all x2 -> x0, waiting for transfers between devices: 9.36 us -> none  [the longest x1 6.77 us: local(): lax.all_to_all(send_rows.reshape(owners, capacity, 2 * width_low), 'blk',...]
    unnamed x20 -> x4, local copies, waits for them, and re-layouts: 0.09 us -> 7.88 us
    slice x3 -> x0, local copies, waits for them, and re-layouts: 3.37 us -> none  [the longest x2 2.59 us: local(): inputs_recv = recv_rows[:, width_low:]]
  transfers between devices with their start and end apart: 13 -> 0, of which waited for: 8 -> 0; matrix products, arithmetic and copies ran while one was open for 6% -> 0% of each run, Pallas kernels for 0% -> 0%
where the time goes in v1:
time: 87.4 us; the launch traced here: 86.8 us
  Pallas kernels  78.9 us (90%)
  local copies, waits for them, and re-layouts  7.88 us (9%)
    pallas_call x1, Pallas kernels, influence_of(): pl.pallas_call(functools.partial(kernel, owners), out_shape=jax.ShapeDtyp...  37 us
    pallas_call x1, Pallas kernels, make_queries(): pl.pallas_call(queries_kernel, out_shape=jax.ShapeDtypeStruct((DOC_DEV, w...  26.6 us
    pallas_call x1, Pallas kernels, dispatch(): pl.pallas_call(functools.partial(dispatch_kernel, owners, capacity), out_...  15.3 us
    unnamed x4, local copies, waits for them, and re-layouts  7.88 us

profile of v1, /device:TPU:0, one launch (start us, length us, event | category | flops | bytes accessed | tf_op | source)
XLA Modules:
  0.0 86.8 jit_solution(11368352761663376217)
XLA Ops:
  0.0 1.5 %copy.10.owner_col = s32[256,1]{1,0:T(8,128)} copy(s32[256,1]{0,1:T(1,128)} %param.12) | data formatting | bytes 2048 | tf_op args[5]
  1.5 2.4 %copy.8.p_in = bf16[4096,64]{1,0:T(8,128)(2,1)} copy(bf16[4096,64]{0,1:T(8,128)(2,1)} %param.9) | data formatting | bytes 1048576 | tf_op args[2]
  3.8 2.4 %copy.9.p_out = bf16[4096,64]{1,0:T(8,128)(2,1)} copy(bf16[4096,64]{0,1:T(8,128)(2,1)} %param.10) | data formatting | bytes 1048576 | tf_op args[3]
  6.3 15.3 %dispatch.1 = (bf16[16,64,128]{2,1,0:T(8,128)(2,1)}, s32[16,1,128]{2,1,0:T(1,128)}) custom-call(bf16[256,4096]{1,0:T(8,128)(2,1)} %x_in.1, bf16[256,4096]{1,0:T(8,128)(2,1)} %x_grad.1, bf16[4096,64]{1,0:T(8,128)(2,1)} %copy.8.p_in, bf16[4096,64]{1,0:T(8,128)(2,1)} %copy.9.p_out, s32[256,1]{1,0:T(8,128)} %copy.10.owner_col, s32[1,256]{1,0:T(1,128)} %bitcast.2, ...), custom_call_target="tpu_custom_call" | custom-call | tf_op jit(solution)/shard_map/dispatch/pallas_call | solution.py:116
  21.6 26.6 %queries.1 = bf16[32,4096]{1,0:T(8,128)(2,1)} custom-call(bf16[16,64,128]{2,1,0:T(8,128)(2,1)} %get-tuple-element.7.recv_rows, s32[16,1,128]{2,1,0:T(1,128)} %get-tuple-element.8.recv_slot), custom_call_target="tpu_custom_call" | custom-call | tf_op jit(solution)/shard_map/queries/pallas_call | solution.py:209
  48.2 37.0 %influence.1 = bf16[12,32,256]{2,1,0:T(8,128)(2,1)} custom-call(bf16[32,4096]{1,0:T(8,128)(2,1)} %queries.1, bf16[256,4096]{1,0:T(8,128)(2,1)} %train.1), custom_call_target="tpu_custom_call" | custom-call | tf_op jit(solution)/shard_map/influence/pallas_call | solution.py:365
  85.2 1.6 %copy.12 = bf16[12,32,256]{2,1,0:T(8,128)(2,1)} copy(bf16[12,32,256]{2,1,0:T(8,128)(2,1)} %influence.1) | data formatting | bytes 393216

commit v2 on v1

v2 whole, which is shorter than its diff:
```python
import functools

import jax
import jax.numpy as jnp
from jax import lax
from jax.experimental import pallas as pl
from jax.experimental.pallas import tpu as pltpu
from jax.sharding import PartitionSpec as P

DOC_DEV = 32
STOPS = 12
NEWTON_STEPS = 6
LEAD = 5
LANES = 128
DOC_GROUP = 8
GROUPS = DOC_DEV // DOC_GROUP
MESH = pl.DeviceIdType.MESH
VMEM_SPEC = pl.BlockSpec(memory_space=pltpu.VMEM)
F32 = jnp.float32
BF16 = jnp.bfloat16
CONTRACT_LAST = (((1,), (1,)), ((), ()))


def matmul(left, right):
    return jnp.dot(left, right, preferred_element_type=F32)


def halves(value):
    high = value.astype(BF16)
    return high, (value - high.astype(F32)).astype(BF16)


def split_matmul(left, right):
    left_high, left_low = left
    right_high, right_low = right
    joined = matmul(
        jnp.concatenate([left_high, left_low], axis=1),
        jnp.concatenate([right_high, right_high], axis=0),
    )
    return joined + matmul(left_high, right_low)


def dispatch_kernel(owners, capacity, x_in, x_grad, p_in, p_out, owner_row, slot_row,
                    recv_rows, recv_slot, low, send_rows, send_slot,
                    rows_sent, rows_here, slot_sent, slot_here):
    me = lax.axis_index("blk")
    barrier = pltpu.get_barrier_semaphore()

    @pl.loop(1, owners)
    def _(ahead):
        pl.semaphore_signal(
            barrier, inc=1, device_id={"blk": lax.rem(me + ahead, owners)}, device_id_type=MESH
        )

    count = x_in.shape[0]
    width = p_in.shape[0]
    for at, values, weights in ((0, x_grad, p_out), (width, x_in, p_in)):
        low[:, at:at + width] = lax.dot_general(
            values[...], weights[...], CONTRACT_LAST, preferred_element_type=F32
        ).astype(BF16)
    token = lax.broadcasted_iota(jnp.int32, (count, count), 0)
    other = lax.broadcasted_iota(jnp.int32, (count, count), 1)
    earlier = jnp.where(token < other, 1.0, 0.0).astype(BF16)
    owner_id = lax.broadcasted_iota(jnp.int32, (owners, count), 0)
    owner_hot = jnp.where(owner_id == owner_row[...], 1.0, 0.0)
    before = matmul(owner_hot.astype(BF16), earlier)
    rank = jnp.sum(before * owner_hot, axis=0, keepdims=True).astype(jnp.int32)
    position = owner_row[...] * capacity + rank
    place = lax.broadcasted_iota(jnp.int32, (owners * capacity, count), 0)
    placed = jnp.where(place == position, 1.0, 0.0).astype(BF16)
    send_rows[...] = matmul(placed, low[...]).astype(BF16).reshape(send_rows.shape)
    coded = jnp.where(owner_id == owner_row[...], slot_row[...] + 1, 0).astype(F32).astype(BF16)
    lane = lax.broadcasted_iota(jnp.int32, (LANES, count), 0)
    shift = lax.rem(me, LANES // capacity) * capacity
    spread = jnp.where(lane == rank + shift, 1.0, 0.0).astype(BF16)
    codes = lax.dot_general(coded, spread, CONTRACT_LAST, preferred_element_type=F32)
    codes = codes.astype(jnp.int32)
    for owner in range(owners):
        send_slot[owner] = codes[owner:owner + 1]
    pl.semaphore_wait(barrier, owners - 1)

    def copies(target, source, sem):
        to = {"blk": target}
        return (
            pltpu.make_async_remote_copy(
                src_ref=send_rows.at[target], dst_ref=recv_rows.at[source],
                send_sem=rows_sent.at[target], recv_sem=rows_here.at[sem],
                device_id=to, device_id_type=MESH),
            pltpu.make_async_remote_copy(
                src_ref=send_slot.at[target], dst_ref=recv_slot.at[source],
                send_sem=slot_sent.at[target], recv_sem=slot_here.at[sem],
                device_id=to, device_id_type=MESH),
        )

    @pl.loop(1, owners)
    def _(ahead):
        for copy in copies(lax.rem(me + ahead, owners), me, me):
            copy.start()

    recv_rows[me] = send_rows[me]
    recv_slot[me] = send_slot[me]

    @pl.loop(1, owners)
    def _(ahead):
        source = lax.rem(me + ahead, owners)
        for copy in copies(source, source, source):
            copy.wait_recv()

    @pl.loop(1, owners)
    def _(ahead):
        for copy in copies(lax.rem(me + ahead, owners), me, me):
            copy.wait_send()


def dispatch(x_in, x_grad, p_in, p_out, owner_row, slot_row):
    owners = lax.axis_size("blk")
    count, width = x_in.shape[0], p_in.shape[0]
    capacity = 4 * count // owners
    rows = (owners, capacity, 2 * width)
    slots = (owners, 1, LANES)
    return pl.pallas_call(
        functools.partial(dispatch_kernel, owners, capacity),
        out_shape=(jax.ShapeDtypeStruct(rows, BF16), jax.ShapeDtypeStruct(slots, jnp.int32)),
        in_specs=[VMEM_SPEC] * 6,
        out_specs=(VMEM_SPEC, VMEM_SPEC),
        scratch_shapes=[
            pltpu.VMEM((count, 2 * width), BF16),
            pltpu.VMEM(rows, BF16),
            pltpu.VMEM(slots, jnp.int32),
        ] + [pltpu.SemaphoreType.DMA((owners,))] * 4,
        compiler_params=pltpu.CompilerParams(collective_id=0, has_side_effects=True),
        name="dispatch",
    )(x_in, x_grad, p_in, p_out, owner_row, slot_row)


def prepare(recv_rows, recv_slot, turned, codes):
    owners, capacity, full = recv_rows.shape
    total = owners * capacity
    group = LANES // capacity
    rows = recv_rows[...].reshape(total, full)
    for part in range(total // LANES):
        span = slice(part * LANES, (part + 1) * LANES)
        turned[:, span] = rows[span].T
        code = recv_slot[part * group]
        for source in range(part * group + 1, (part + 1) * group):
            code = code + recv_slot[source]
        codes[:, span] = code


def query_group(step, recv_rows, turned, codes, flat, out):
    owners, capacity, full = recv_rows.shape
    width = full // 2
    row = lax.broadcasted_iota(jnp.int32, (full, full), 0)
    col = lax.broadcasted_iota(jnp.int32, (full, full), 1)
    upper_row = row < width
    diagonal = upper_row == (col < width)
    corner = upper_row & (col >= width)
    identity_mat = jnp.where(row == col, 1.0, 0.0)
    upper = lax.broadcasted_iota(jnp.int32, (full, 1), 0) < width
    docs = range(DOC_GROUP)
    code = codes[...]
    counts, masked = [], []
    for doc in docs:
        hot = jnp.where(code == step * DOC_GROUP + doc + 1, 1.0, 0.0)
        counts.append(jnp.sum(hot, axis=1, keepdims=True))
        masked.append(turned[...] * hot.astype(BF16))
    rows = recv_rows[...].reshape(owners * capacity, full)
    grams = matmul(jnp.concatenate(masked, axis=0), rows)
    grams = [grams[doc * full:(doc + 1) * full] for doc in docs]
    powers, approx = [], []
    for doc in docs:
        damped = jnp.where(diagonal, grams[doc] / (counts[doc] + 1.0), 0.0) + identity_mat
        sums = jnp.sum(jnp.abs(damped), axis=1, keepdims=True)
        bound = jnp.where(
            upper,
            jnp.max(sums[:width], axis=0, keepdims=True),
            jnp.max(sums[width:], axis=0, keepdims=True),
        )
        scale = 1.0 / bound
        residual = identity_mat - damped * scale
        approx.append((identity_mat + residual) * scale)
        parts = halves(residual)
        powers.append(split_matmul(parts, parts))
    for level in range(NEWTON_STEPS - 2):
        for doc in docs:
            power = halves(powers[doc])
            inverse = halves(approx[doc])
            both = tuple(jnp.concatenate([p, x], axis=1) for p, x in zip(power, inverse))
            product = split_matmul(power, both)
            powers[doc] = product[:, :full]
            approx[doc] = approx[doc] + product[:, full:]
    for doc in docs:
        inverse = approx[doc] + split_matmul(halves(powers[doc]), halves(approx[doc]))
        mixed = jnp.where(corner, grams[doc], 0.0)
        tilted = split_matmul(halves(inverse[:width]), halves(mixed))
        right = inverse[width:]
        right = right + pltpu.roll(right, width, 1)
        right = jnp.concatenate([jnp.zeros_like(right), right], axis=0)
        flat[doc * width:(doc + 1) * width, :] = split_matmul(halves(tilted), halves(right))

    left = lax.broadcasted_iota(jnp.int32, (DOC_GROUP, full), 1) < width
    for pair in range(width // 2):
        even = flat[pl.ds(2 * pair, DOC_GROUP, stride=width), :]
        odd = flat[pl.ds(2 * pair + 1, DOC_GROUP, stride=width), :]
        out[:, pair * full:(pair + 1) * full] = jnp.where(left, even, odd).astype(BF16)


def query_scratch(recv_rows):
    owners, capacity, full = recv_rows.shape
    total = owners * capacity
    return [
        pltpu.VMEM((full, total), BF16),
        pltpu.VMEM((1, total), jnp.int32),
        pltpu.VMEM((DOC_GROUP * (full // 2), full), F32),
    ]


def queries_kernel(recv_rows, recv_slot, out, turned, codes, flat):
    prepare(recv_rows, recv_slot, turned, codes)

    @pl.loop(0, GROUPS)
    def _(step):
        query_group(step, recv_rows, turned, codes, flat, out.at[step])


def make_queries(recv_rows, recv_slot):
    width = recv_rows.shape[2] // 2
    return pl.pallas_call(
        queries_kernel,
        out_shape=jax.ShapeDtypeStruct((GROUPS, DOC_GROUP, width * width), BF16),
        in_specs=[VMEM_SPEC] * 2,
        out_specs=VMEM_SPEC,
        scratch_shapes=query_scratch(recv_rows),
        name="queries",
    )(recv_rows, recv_slot).reshape(DOC_DEV, width * width)


def score_into(out, index, block, train):
    out[index] = lax.dot_general(
        block[...], train[...], CONTRACT_LAST, preferred_element_type=F32
    ).astype(BF16)


def window_kernel(owners, queries, train, out, held, sent, here):
    me = lax.axis_index("blk")
    barrier = pltpu.get_barrier_semaphore()

    def peer(stop):
        return lax.rem(me + stop - LEAD + owners, owners)

    def source(stop):
        return lax.rem(me - stop + LEAD + owners, owners)

    def copy(stop):
        return pltpu.make_async_remote_copy(
            src_ref=queries, dst_ref=held.at[stop], send_sem=sent.at[stop],
            recv_sem=here.at[stop], device_id={"blk": peer(stop)}, device_id_type=MESH)

    others = [stop for stop in range(STOPS) if stop != LEAD]
    for stop in others:
        pl.semaphore_signal(
            barrier, inc=1, device_id={"blk": source(stop)}, device_id_type=MESH
        )
    pl.semaphore_wait(barrier, len(others))
    for stop in others:
        copy(stop).start()
    score_into(out, LEAD, queries, train)
    for stop in others:
        copy(stop).wait_recv()
        score_into(out, stop, held.at[stop], train)
    for stop in others:
        copy(stop).wait_send()


def grid_kernel(owners, recv_rows, recv_slot, train, out, turned, codes, flat, held,
                up_sent, down_sent, side_sent, twin_sent, here):
    lines = owners // 4
    me = lax.axis_index("blk")
    core = lax.rem(me, 2)
    side = lax.rem(me // 2, 2)
    line = me // 4
    twin = me + 1 - 2 * core
    across = me + 2 - 4 * side
    across_twin = across + 1 - 2 * core
    above, below = me + 4, me - 4
    has_up, has_down = line + 1 < lines, line > 0

    def stop_of(device, origin):
        return lax.rem(device - origin + LEAD + owners, owners)

    def wants(device, origin):
        return stop_of(device, origin) < STOPS

    def copy(group, origin, sems, device):
        mine, theirs = stop_of(me, origin), stop_of(device, origin)
        return pltpu.make_async_remote_copy(
            src_ref=held.at[group, mine], dst_ref=held.at[group, theirs],
            send_sem=sems.at[group, mine], recv_sem=here.at[group, theirs],
            device_id={"blk": device}, device_id_type=MESH)

    def arrive(group, origin):
        mine = stop_of(me, origin)
        pltpu.make_async_remote_copy(
            src_ref=held.at[group, mine], dst_ref=held.at[group, mine],
            send_sem=twin_sent.at[group, mine], recv_sem=here.at[group, mine],
            device_id={"blk": twin}, device_id_type=MESH).wait_recv()

    barrier = pltpu.get_barrier_semaphore()

    def greet(device):
        pl.semaphore_signal(barrier, inc=1, device_id={"blk": device}, device_id_type=MESH)

    greet(twin)
    greet(across)
    pl.when(has_up)(lambda: greet(above))
    pl.when(has_down)(lambda: greet(below))
    prepare(recv_rows, recv_slot, turned, codes)

    def candidate(stage, index):
        way, column, plane = lax.rem(index, 2), lax.rem(index // 2, 2), index // 4
        distance = stage - column
        spot = line + distance * (2 * way - 1)
        near = lax.rem(side + column, 2)
        origin = (spot * 2 + near) * 2 + lax.rem(core + plane, 2)
        real = (spot >= 0) & (spot < lines) & (distance >= 0)
        real = real & ((distance > 0) | (way == 0))
        return way, column, origin, real

    def comes(column, origin, real):
        return real & ((column == 0) | wants(me, origin) | wants(twin, origin))

    def passes(group, stage, index, act):
        way, column, origin, real = candidate(stage, index)
        straight = real & (column == 0)
        pl.when(straight & ((way == 0) | (stage == 0)) & has_up)(
            lambda: act(copy(group, origin, up_sent, above)))
        pl.when(straight & ((way == 1) | (stage == 0)) & has_down)(
            lambda: act(copy(group, origin, down_sent, below)))
        pl.when(straight & (wants(across, origin) | wants(across_twin, origin)))(
            lambda: act(copy(group, origin, side_sent, across)))
        pl.when(comes(column, origin, real) & wants(twin, origin))(
            lambda: act(copy(group, origin, twin_sent, twin)))

    @pl.loop(0, GROUPS + lines)
    def _(step):
        @pl.when(step < GROUPS)
        def _():
            query_group(step, recv_rows, turned, codes, flat, held.at[step, LEAD])

            @pl.when(step == 0)
            def _():
                pl.semaphore_wait(barrier, 2 + has_up.astype(jnp.int32) + has_down.astype(jnp.int32))

            passes(step, 0, 0, lambda c: c.start())

        @pl.loop(0, lines)
        def _(back):
            stage = lines - back
            group = step - stage

            @pl.when((group >= 0) & (group < GROUPS))
            def _():
                @pl.loop(0, 4)
                def _(index):
                    _, column, origin, real = candidate(stage, index)

                    @pl.when(comes(column, origin, real))
                    def _():
                        arrive(group, origin)

                    passes(group, stage, index, lambda c: c.start())

        @pl.when(step >= lines)
        def _():
            group = step - lines

            @pl.loop(0, lines + 1)
            def _(stage):
                @pl.loop(4, 8)
                def _(index):
                    _, _, origin, real = candidate(stage, index)

                    @pl.when(real & wants(me, origin))
                    def _():
                        arrive(group, origin)

            block = held[group, :STOPS].reshape(STOPS * DOC_GROUP, train.shape[1])
            tile = lax.dot_general(block, train[...], CONTRACT_LAST, preferred_element_type=F32)
            out[group] = tile.astype(BF16).reshape(STOPS, DOC_GROUP, train.shape[0])

    @pl.loop(0, GROUPS)
    def _(group):
        passes(group, 0, 0, lambda c: c.wait_send())

        @pl.loop(1, lines + 1)
        def _(stage):
            @pl.loop(0, 4)
            def _(index):
                passes(group, stage, index, lambda c: c.wait_send())


def influence_of(recv_rows, recv_slot, train):
    owners = lax.axis_size("blk")
    params = pltpu.CompilerParams(collective_id=1, has_side_effects=True)
    if owners % 4 == 0 and owners < 2 * STOPS:
        tiles = pl.pallas_call(
            functools.partial(grid_kernel, owners),
            out_shape=jax.ShapeDtypeStruct((GROUPS, STOPS, DOC_GROUP, train.shape[0]), BF16),
            in_specs=[VMEM_SPEC] * 3,
            out_specs=VMEM_SPEC,
            scratch_shapes=query_scratch(recv_rows)
            + [pltpu.VMEM((GROUPS, owners, DOC_GROUP, train.shape[1]), BF16)]
            + [pltpu.SemaphoreType.DMA((GROUPS, owners))] * 5,
            compiler_params=params,
            name="influence",
        )(recv_rows, recv_slot, train)
        return tiles.transpose(1, 0, 2, 3).reshape(STOPS, DOC_DEV, train.shape[0])
    queries = make_queries(recv_rows, recv_slot)
    return pl.pallas_call(
        functools.partial(window_kernel, owners),
        out_shape=jax.ShapeDtypeStruct((STOPS, DOC_DEV, train.shape[0]), BF16),
        in_specs=[VMEM_SPEC] * 2,
        out_specs=VMEM_SPEC,
        scratch_shapes=[pltpu.VMEM((STOPS,) + queries.shape, BF16)]
        + [pltpu.SemaphoreType.DMA((STOPS,))] * 2,
        compiler_params=params,
        name="influence",
    )(queries, train)


def local(query_inputs, query_grads, proj_in, proj_out, train_rows, token_owner, token_slot):
    recv_rows, recv_slot = dispatch(
        query_inputs, query_grads, proj_in.T, proj_out.T,
        token_owner.reshape(1, -1), token_slot.reshape(1, -1),
    )
    return influence_of(recv_rows, recv_slot, train_rows)


def solution(mesh):
    placed = (
        P(("groups", "blk"), None),
        P(("groups", "blk"), None),
        P(),
        P(),
        P(("groups", "blk"), None),
        P(("groups", "blk"), None),
        P(("groups", "blk")),
    )
    return jax.shard_map(
        local,
        mesh=mesh,
        in_specs=placed,
        out_specs=P(None, None, ("groups", "blk")),
        check_vma=False,
    )
```

time: 87.4 us -> 69.1 us (0.79)
  Pallas kernels: 78.9 us -> 66.8 us
  local copies, waits for them, and re-layouts: 7.88 us -> 1.62 us
    pallas_call x2 -> x1, Pallas kernels: 63.6 us -> 51.9 us  [influence_of(): pl.pallas_call(functools.partial(grid_kernel, owners), out_shape=jax.Shap...]
    unnamed x4 -> x0, local copies, waits for them, and re-layouts: 7.88 us -> none
    reshape x0 -> x1, local copies, waits for them, and re-layouts: none -> 1.62 us  [influence_of(): return tiles.transpose(1, 0, 2, 3).reshape(STOPS, DOC_DEV, train.shape[0])]
where the time goes in v2:
time: 69.1 us; the launch traced here: 68.5 us
  Pallas kernels  66.8 us (97%)
  local copies, waits for them, and re-layouts  1.62 us (2%)
    pallas_call x1, Pallas kernels, influence_of(): pl.pallas_call(functools.partial(grid_kernel, owners), out_shape=jax.Shap...  51.9 us
    pallas_call x1, Pallas kernels, dispatch(): pl.pallas_call(functools.partial(dispatch_kernel, owners, capacity), out_...  14.9 us
    reshape x1, local copies, waits for them, and re-layouts, influence_of(): return tiles.transpose(1, 0, 2, 3).reshape(STOPS, DOC_DEV, train.shape[0])  1.62 us

profile of v2, /device:TPU:0, one launch (start us, length us, event | category | flops | bytes accessed | tf_op | source)
XLA Modules:
  0.0 68.5 jit_solution(11272242176851054931)
XLA Ops:
  0.0 14.9 %dispatch.1 = (bf16[16,64,128]{2,1,0:T(8,128)(2,1)}, s32[16,1,128]{2,1,0:T(1,128)}) custom-call(bf16[256,4096]{1,0:T(8,128)(2,1)} %x_in.1, bf16[256,4096]{1,0:T(8,128)(2,1)} %x_grad.1, bf16[64,4096]{1,0:T(8,128)(2,1)} %bitcast.9, bf16[64,4096]{1,0:T(8,128)(2,1)} %bitcast.10, s32[1,256]{1,0:T(1,128)} %bitcast.11, s32[1,256]{1,0:T(1,128)} %bitcast.12), custom_call_target="tpu_custom_call" | custom-call | tf_op jit(solution)/shard_map/dispatch/pallas_call | solution.py:121
  14.9 51.9 %influence.1 = bf16[4,12,8,256]{3,2,1,0:T(8,128)(2,1)} custom-call(bf16[16,64,128]{2,1,0:T(8,128)(2,1)} %get-tuple-element.7.recv_rows, s32[16,1,128]{2,1,0:T(1,128)} %get-tuple-element.8.recv_slot, bf16[256,4096]{1,0:T(8,128)(2,1)} %train.1), custom_call_target="tpu_custom_call" | custom-call | tf_op jit(solution)/shard_map/influence/pallas_call | solution.py:406
  66.8 1.6 %copy_bitcast_fusion = bf16[12,32,256]{2,1,0:T(8,128)(2,1)} fusion(bf16[4,12,8,256]{3,2,1,0:T(8,128)(2,1)} %influence.1), kind=kLoop, calls=%fused_computation | loop fusion | bytes 393216 | tf_op jit(solution)/shard_map/reshape | solution.py:417

commit v3 on v2

--- a/solution.py
+++ b/solution.py
@@ -30,14 +30,28 @@
     return high, (value - high.astype(F32)).astype(BF16)
 
 
-def split_matmul(left, right):
-    left_high, left_low = left
-    right_high, right_low = right
-    joined = matmul(
-        jnp.concatenate([left_high, left_low], axis=1),
-        jnp.concatenate([right_high, right_high], axis=0),
+def left_parts(value, right_half):
+    width = value.shape[1] // 2
+    high = value.astype(BF16).astype(F32)
+    low = value - high
+    if right_half:
+        high = pltpu.roll(high, width, 1)
+    else:
+        low = pltpu.roll(low, width, 1)
+    is_left = lax.broadcasted_iota(jnp.int32, value.shape, 1) < width
+    parts = jnp.where(is_left, high, low).astype(BF16)
+    return jnp.concatenate([parts, parts], axis=1)
+
+
+def pair_product(lefts, rights, right_half):
+    high, low = zip(*[halves(value) for value in rights])
+    high, low = jnp.concatenate(high, axis=1), jnp.concatenate(low, axis=1)
+    product = matmul(
+        jnp.concatenate([left_parts(value, right_half) for value in lefts], axis=0),
+        jnp.concatenate([high, high, low, low], axis=0),
     )
-    return joined + matmul(left_high, right_low)
+    rows, cols = lefts[0].shape
+    return product[:rows, :cols], product[rows:, cols:]
 
 
 def dispatch_kernel(owners, capacity, x_in, x_grad, p_in, p_out, owner_row, slot_row,
@@ -150,13 +164,11 @@
 def query_group(step, recv_rows, turned, codes, flat, out):
     owners, capacity, full = recv_rows.shape
     width = full // 2
-    row = lax.broadcasted_iota(jnp.int32, (full, full), 0)
-    col = lax.broadcasted_iota(jnp.int32, (full, full), 1)
-    upper_row = row < width
-    diagonal = upper_row == (col < width)
-    corner = upper_row & (col >= width)
-    identity_mat = jnp.where(row == col, 1.0, 0.0)
-    upper = lax.broadcasted_iota(jnp.int32, (full, 1), 0) < width
+    row = lax.broadcasted_iota(jnp.int32, (width, full), 0)
+    col = lax.broadcasted_iota(jnp.int32, (width, full), 1)
+    left = col < width
+    left_eye = jnp.where(row == col, 1.0, 0.0)
+    right_eye = jnp.where(row + width == col, 1.0, 0.0)
     docs = range(DOC_GROUP)
     code = codes[...]
     counts, masked = [], []
@@ -166,43 +178,39 @@
         masked.append(turned[...] * hot.astype(BF16))
     rows = recv_rows[...].reshape(owners * capacity, full)
     grams = matmul(jnp.concatenate(masked, axis=0), rows)
-    grams = [grams[doc * full:(doc + 1) * full] for doc in docs]
-    powers, approx = [], []
+    crossed, states = [], []
     for doc in docs:
-        damped = jnp.where(diagonal, grams[doc] / (counts[doc] + 1.0), 0.0) + identity_mat
-        sums = jnp.sum(jnp.abs(damped), axis=1, keepdims=True)
-        bound = jnp.where(
-            upper,
-            jnp.max(sums[:width], axis=0, keepdims=True),
-            jnp.max(sums[width:], axis=0, keepdims=True),
-        )
-        scale = 1.0 / bound
-        residual = identity_mat - damped * scale
-        approx.append((identity_mat + residual) * scale)
-        parts = halves(residual)
-        powers.append(split_matmul(parts, parts))
-    for level in range(NEWTON_STEPS - 2):
+        top = grams[doc * full:doc * full + width]
+        bottom = grams[doc * full + width:(doc + 1) * full]
+        crossed.append(top)
+        pair = []
+        for outer in (top, pltpu.roll(bottom, width, 1)):
+            damped = jnp.where(left, outer / (counts[doc] + 1.0), 0.0) + left_eye
+            sums = jnp.sum(jnp.abs(damped), axis=1, keepdims=True)
+            scale = 1.0 / jnp.max(sums, axis=0, keepdims=True)
+            pair.append(left_eye - damped * scale + right_eye * scale)
+        states.append(pair)
+    for level in range(NEWTON_STEPS):
         for doc in docs:
-            power = halves(powers[doc])
-            inverse = halves(approx[doc])
-            both = tuple(jnp.concatenate([p, x], axis=1) for p, x in zip(power, inverse))
-            product = split_matmul(power, both)
-            powers[doc] = product[:, :full]
-            approx[doc] = approx[doc] + product[:, full:]
-    for doc in docs:
-        inverse = approx[doc] + split_matmul(halves(powers[doc]), halves(approx[doc]))
-        mixed = jnp.where(corner, grams[doc], 0.0)
-        tilted = split_matmul(halves(inverse[:width]), halves(mixed))
-        right = inverse[width:]
-        right = right + pltpu.roll(right, width, 1)
-        right = jnp.concatenate([jnp.zeros_like(right), right], axis=0)
-        flat[doc * width:(doc + 1) * width, :] = split_matmul(halves(tilted), halves(right))
-
-    left = lax.broadcasted_iota(jnp.int32, (DOC_GROUP, full), 1) < width
+            products = pair_product(states[doc], states[doc], False)
+            states[doc] = [
+                product + jnp.where(left, 0.0, state)
+                for product, state in zip(products, states[doc])
+            ]
+    for doc in range(0, DOC_GROUP, 2):
+        pair = (doc, doc + 1)
+        tilted = pair_product(
+            [states[d][0] for d in pair], [crossed[d] for d in pair], True)
+        tilted = pair_product(tilted, [states[d][1] for d in pair], True)
+        for d, value in zip(pair, tilted):
+            flat[d * width:(d + 1) * width, :] = value
+
+    near = lax.broadcasted_iota(jnp.int32, (DOC_GROUP, full), 1) < width
     for pair in range(width // 2):
         even = flat[pl.ds(2 * pair, DOC_GROUP, stride=width), :]
         odd = flat[pl.ds(2 * pair + 1, DOC_GROUP, stride=width), :]
-        out[:, pair * full:(pair + 1) * full] = jnp.where(left, even, odd).astype(BF16)
+        both = jnp.where(near, pltpu.roll(even, width, 1), odd)
+        out[:, pair * full:(pair + 1) * full] = both.astype(BF16)
 
 
 def query_scratch(recv_rows):
@@ -281,29 +289,9 @@
     line = me // 4
     twin = me + 1 - 2 * core
     across = me + 2 - 4 * side
-    across_twin = across + 1 - 2 * core
+    to_twin, to_across = 1 - 2 * core, 2 - 4 * side
     above, below = me + 4, me - 4
     has_up, has_down = line + 1 < lines, line > 0
-
-    def stop_of(device, origin):
-        return lax.rem(device - origin + LEAD + owners, owners)
-
-    def wants(device, origin):
-        return stop_of(device, origin) < STOPS
-
-    def copy(group, origin, sems, device):
-        mine, theirs = stop_of(me, origin), stop_of(device, origin)
-        return pltpu.make_async_remote_copy(
-            src_ref=held.at[group, mine], dst_ref=held.at[group, theirs],
-            send_sem=sems.at[group, mine], recv_sem=here.at[group, theirs],
-            device_id={"blk": device}, device_id_type=MESH)
-
-    def arrive(group, origin):
-        mine = stop_of(me, origin)
-        pltpu.make_async_remote_copy(
-            src_ref=held.at[group, mine], dst_ref=held.at[group, mine],
-            send_sem=twin_sent.at[group, mine], recv_sem=here.at[group, mine],
-            device_id={"blk": twin}, device_id_type=MESH).wait_recv()
 
     barrier = pltpu.get_barrier_semaphore()
 
@@ -316,30 +304,75 @@
     pl.when(has_down)(lambda: greet(below))
     prepare(recv_rows, recv_slot, turned, codes)
 
-    def candidate(stage, index):
-        way, column, plane = lax.rem(index, 2), lax.rem(index // 2, 2), index // 4
+    def wrapped(stop):
+        return stop % owners if isinstance(stop, int) else lax.rem(stop + 3 * owners, owners)
+
+    def wanted(stop):
+        return wrapped(stop) < STOPS
+
+    def either(first, second):
+        return True if first is True or second is True else first | second
+
+    def both(first, second):
+        if first is True or second is True:
+            return second if first is True else first
+        return first & second
+
+    def when(wish, act):
+        if wish is True:
+            act()
+        elif wish is not False:
+            pl.when(wish)(act)
+
+    def reached(distance, way):
+        if distance == 0:
+            return True
+        return line >= distance if way == 0 else line < lines - distance
+
+    def place(stage, way, column):
         distance = stage - column
-        spot = line + distance * (2 * way - 1)
-        near = lax.rem(side + column, 2)
-        origin = (spot * 2 + near) * 2 + lax.rem(core + plane, 2)
-        real = (spot >= 0) & (spot < lines) & (distance >= 0)
-        real = real & ((distance > 0) | (way == 0))
-        return way, column, origin, real
-
-    def comes(column, origin, real):
-        return real & ((column == 0) | wants(me, origin) | wants(twin, origin))
-
-    def passes(group, stage, index, act):
-        way, column, origin, real = candidate(stage, index)
-        straight = real & (column == 0)
-        pl.when(straight & ((way == 0) | (stage == 0)) & has_up)(
-            lambda: act(copy(group, origin, up_sent, above)))
-        pl.when(straight & ((way == 1) | (stage == 0)) & has_down)(
-            lambda: act(copy(group, origin, down_sent, below)))
-        pl.when(straight & (wants(across, origin) | wants(across_twin, origin)))(
-            lambda: act(copy(group, origin, side_sent, across)))
-        pl.when(comes(column, origin, real) & wants(twin, origin))(
-            lambda: act(copy(group, origin, twin_sent, twin)))
+        if distance < 0 or (distance == 0 and way == 1):
+            return None
+        stop = LEAD - 4 * distance * (2 * way - 1)
+        if column:
+            stop = stop - to_across
+        real = reached(distance, way)
+        hands = []
+        if column == 0:
+            if way == 0:
+                hands.append((both(real, has_up), 0, above, stop + 4))
+            if way == 1 or distance == 0:
+                hands.append((both(real, has_down), 1, below, stop - 4))
+            sideways = either(wanted(stop + to_across), wanted(stop + to_across + to_twin))
+            if distance == 0:
+                sideways = True
+            hands.append((both(real, sideways), 2, across, stop + to_across))
+        else:
+            real = both(real, either(wanted(stop), wanted(stop + to_twin)))
+        hands.append((both(real, wanted(stop + to_twin)), 3, twin, stop + to_twin))
+        twin_stop = stop - to_twin
+        from_twin = both(reached(distance, way), wanted(twin_stop))
+        hands = [(wish, sem, device, wrapped(theirs)) for wish, sem, device, theirs in hands]
+        return wrapped(stop), real, hands, wrapped(twin_stop), from_twin
+
+    sems = (up_sent, down_sent, side_sent, twin_sent)
+    stages = []
+    for stage in range(lines + 1):
+        found = [place(stage, way, column) for column in range(2) for way in range(2)]
+        stages.append([item for item in found if item is not None])
+
+    def copy(group, mine, sem, device, theirs):
+        return pltpu.make_async_remote_copy(
+            src_ref=held.at[group, mine], dst_ref=held.at[group, theirs],
+            send_sem=sems[sem].at[group, mine], recv_sem=here.at[group, theirs],
+            device_id={"blk": device}, device_id_type=MESH)
+
+    def arrive(group, mine):
+        copy(group, mine, 3, twin, mine).wait_recv()
+
+    def hand_on(group, item):
+        for wish, sem, device, theirs in item[2]:
+            when(wish, lambda: copy(group, item[0], sem, device, theirs).start())
 
     @pl.loop(0, GROUPS + lines)
     def _(step):
@@ -351,52 +384,33 @@
             def _():
                 pl.semaphore_wait(barrier, 2 + has_up.astype(jnp.int32) + has_down.astype(jnp.int32))
 
-            passes(step, 0, 0, lambda c: c.start())
-
-        @pl.loop(0, lines)
-        def _(back):
-            stage = lines - back
+            hand_on(step, stages[0][0])
+
+        for stage in range(lines, 0, -1):
             group = step - stage
 
             @pl.when((group >= 0) & (group < GROUPS))
             def _():
-                @pl.loop(0, 4)
-                def _(index):
-                    _, column, origin, real = candidate(stage, index)
-
-                    @pl.when(comes(column, origin, real))
-                    def _():
-                        arrive(group, origin)
-
-                    passes(group, stage, index, lambda c: c.start())
+                for item in stages[stage]:
+                    when(item[1], lambda: arrive(group, item[0]))
+                    hand_on(group, item)
 
         @pl.when(step >= lines)
         def _():
             group = step - lines
-
-            @pl.loop(0, lines + 1)
-            def _(stage):
-                @pl.loop(4, 8)
-                def _(index):
-                    _, _, origin, real = candidate(stage, index)
-
-                    @pl.when(real & wants(me, origin))
-                    def _():
-                        arrive(group, origin)
-
+            for items in stages:
+                for _, _, _, twin_stop, from_twin in items:
+                    when(from_twin, lambda: arrive(group, twin_stop))
             block = held[group, :STOPS].reshape(STOPS * DOC_GROUP, train.shape[1])
             tile = lax.dot_general(block, train[...], CONTRACT_LAST, preferred_element_type=F32)
             out[group] = tile.astype(BF16).reshape(STOPS, DOC_GROUP, train.shape[0])
 
     @pl.loop(0, GROUPS)
     def _(group):
-        passes(group, 0, 0, lambda c: c.wait_send())
-
-        @pl.loop(1, lines + 1)
-        def _(stage):
-            @pl.loop(0, 4)
-            def _(index):
-                passes(group, stage, index, lambda c: c.wait_send())
+        for items in stages:
+            for item in items:
+                for wish, sem, device, theirs in item[2]:
+                    when(wish, lambda: copy(group, item[0], sem, device, theirs).wait_send())
 
 
 def influence_of(recv_rows, recv_slot, train):

time: 69.1 us -> 59.7 us (0.86)
  Pallas kernels: 66.8 us -> 57.1 us
    pallas_call x1, Pallas kernels: 51.9 us -> 42.2 us  [influence_of(): pl.pallas_call(functools.partial(grid_kernel, owners), out_shape=jax.Shap...]
where the time goes in v3:
time: 59.7 us; the launch traced here: 58.7 us
  Pallas kernels  57.1 us (96%)
  local copies, waits for them, and re-layouts  1.62 us (3%)
    pallas_call x1, Pallas kernels, influence_of(): pl.pallas_call(functools.partial(grid_kernel, owners), out_shape=jax.Shap...  42.2 us
    pallas_call x1, Pallas kernels, dispatch(): pl.pallas_call(functools.partial(dispatch_kernel, owners, capacity), out_...  14.9 us
    reshape x1, local copies, waits for them, and re-layouts, influence_of(): return tiles.transpose(1, 0, 2, 3).reshape(STOPS, DOC_DEV, train.shape[0])  1.62 us

profile of v3, /device:TPU:0, one launch (start us, length us, event | category | flops | bytes accessed | tf_op | source)
XLA Modules:
  0.0 58.7 jit_solution(13215682775028351114)
XLA Ops:
  0.0 14.9 %dispatch.1 = (bf16[16,64,128]{2,1,0:T(8,128)(2,1)}, s32[16,1,128]{2,1,0:T(1,128)}) custom-call(bf16[256,4096]{1,0:T(8,128)(2,1)} %x_in.1, bf16[256,4096]{1,0:T(8,128)(2,1)} %x_grad.1, bf16[64,4096]{1,0:T(8,128)(2,1)} %bitcast.9, bf16[64,4096]{1,0:T(8,128)(2,1)} %bitcast.10, s32[1,256]{1,0:T(1,128)} %bitcast.11, s32[1,256]{1,0:T(1,128)} %bitcast.12), custom_call_target="tpu_custom_call" | custom-call | tf_op jit(solution)/shard_map/dispatch/pallas_call | solution.py:135
  14.9 42.2 %influence.1 = bf16[4,12,8,256]{3,2,1,0:T(8,128)(2,1)} custom-call(bf16[16,64,128]{2,1,0:T(8,128)(2,1)} %get-tuple-element.7.recv_rows, s32[16,1,128]{2,1,0:T(1,128)} %get-tuple-element.8.recv_slot, bf16[256,4096]{1,0:T(8,128)(2,1)} %train.1), custom_call_target="tpu_custom_call" | custom-call | tf_op jit(solution)/shard_map/influence/pallas_call | solution.py:420
  57.1 1.6 %copy_bitcast_fusion = bf16[12,32,256]{2,1,0:T(8,128)(2,1)} fusion(bf16[4,12,8,256]{3,2,1,0:T(8,128)(2,1)} %influence.1), kind=kLoop, calls=%fused_computation | loop fusion | bytes 393216 | tf_op jit(solution)/shard_map/reshape | solution.py:431

commit v4 on v3

--- a/solution.py
+++ b/solution.py
@@ -177,11 +177,14 @@
         counts.append(jnp.sum(hot, axis=1, keepdims=True))
         masked.append(turned[...] * hot.astype(BF16))
     rows = recv_rows[...].reshape(owners * capacity, full)
-    grams = matmul(jnp.concatenate(masked, axis=0), rows)
+    half = DOC_GROUP // 2
+    grams = [
+        matmul(jnp.concatenate(masked[at:at + half], axis=0), rows) for at in (0, half)
+    ]
     crossed, states = [], []
     for doc in docs:
-        top = grams[doc * full:doc * full + width]
-        bottom = grams[doc * full + width:(doc + 1) * full]
+        gram = grams[doc // half][doc % half * full:(doc % half + 1) * full]
+        top, bottom = gram[:width], gram[width:]
         crossed.append(top)
         pair = []
         for outer in (top, pltpu.roll(bottom, width, 1)):

time: 59.7 us -> 58.2 us (0.975)
  Pallas kernels: 57.1 us -> 55.6 us
    pallas_call x1, Pallas kernels: 42.2 us -> 40.7 us  [influence_of(): pl.pallas_call(functools.partial(grid_kernel, owners), out_shape=jax.Shap...]
where the time goes in v4:
time: 58.2 us; the launch traced here: 57.3 us
  Pallas kernels  55.6 us (96%)
  local copies, waits for them, and re-layouts  1.62 us (3%)
    pallas_call x1, Pallas kernels, influence_of(): pl.pallas_call(functools.partial(grid_kernel, owners), out_shape=jax.Shap...  40.7 us
    pallas_call x1, Pallas kernels, dispatch(): pl.pallas_call(functools.partial(dispatch_kernel, owners, capacity), out_...  14.9 us
    reshape x1, local copies, waits for them, and re-layouts, influence_of(): return tiles.transpose(1, 0, 2, 3).reshape(STOPS, DOC_DEV, train.shape[0])  1.62 us

profile of v4, /device:TPU:0, one launch (start us, length us, event | category | flops | bytes accessed | tf_op | source)
XLA Modules:
  0.0 57.3 jit_solution(17091670946543290307)
XLA Ops:
  0.0 14.9 %dispatch.1 = (bf16[16,64,128]{2,1,0:T(8,128)(2,1)}, s32[16,1,128]{2,1,0:T(1,128)}) custom-call(bf16[256,4096]{1,0:T(8,128)(2,1)} %x_in.1, bf16[256,4096]{1,0:T(8,128)(2,1)} %x_grad.1, bf16[64,4096]{1,0:T(8,128)(2,1)} %bitcast.9, bf16[64,4096]{1,0:T(8,128)(2,1)} %bitcast.10, s32[1,256]{1,0:T(1,128)} %bitcast.11, s32[1,256]{1,0:T(1,128)} %bitcast.12), custom_call_target="tpu_custom_call" | custom-call | tf_op jit(solution)/shard_map/dispatch/pallas_call | solution.py:135
  14.9 40.7 %influence.1 = bf16[4,12,8,256]{3,2,1,0:T(8,128)(2,1)} custom-call(bf16[16,64,128]{2,1,0:T(8,128)(2,1)} %get-tuple-element.7.recv_rows, s32[16,1,128]{2,1,0:T(1,128)} %get-tuple-element.8.recv_slot, bf16[256,4096]{1,0:T(8,128)(2,1)} %train.1), custom_call_target="tpu_custom_call" | custom-call | tf_op jit(solution)/shard_map/influence/pallas_call | solution.py:423
  55.6 1.6 %copy_bitcast_fusion = bf16[12,32,256]{2,1,0:T(8,128)(2,1)} fusion(bf16[4,12,8,256]{3,2,1,0:T(8,128)(2,1)} %influence.1), kind=kLoop, calls=%fused_computation | loop fusion | bytes 393216 | tf_op jit(solution)/shard_map/reshape | solution.py:434

commit v5 on v4

--- a/solution.py
+++ b/solution.py
@@ -14,6 +14,7 @@
 LANES = 128
 DOC_GROUP = 8
 GROUPS = DOC_DEV // DOC_GROUP
+FIRST_STEPS = 2
 MESH = pl.DeviceIdType.MESH
 VMEM_SPEC = pl.BlockSpec(memory_space=pltpu.VMEM)
 F32 = jnp.float32
@@ -161,7 +162,7 @@
         codes[:, span] = code
 
 
-def query_group(step, recv_rows, turned, codes, flat, out):
+def start_group(step, recv_rows, turned, codes, state):
     owners, capacity, full = recv_rows.shape
     width = full // 2
     row = lax.broadcasted_iota(jnp.int32, (width, full), 0)
@@ -193,17 +194,30 @@
             scale = 1.0 / jnp.max(sums, axis=0, keepdims=True)
             pair.append(left_eye - damped * scale + right_eye * scale)
         states.append(pair)
-    for level in range(NEWTON_STEPS):
-        for doc in docs:
+    for doc, pair in enumerate(newton_steps(states, left, FIRST_STEPS)):
+        state[doc, 0], state[doc, 1], state[doc, 2] = pair[0], pair[1], crossed[doc]
+
+
+def newton_steps(states, left, steps):
+    states = list(states)
+    for level in range(steps):
+        for doc in range(DOC_GROUP):
             products = pair_product(states[doc], states[doc], False)
             states[doc] = [
-                product + jnp.where(left, 0.0, state)
-                for product, state in zip(products, states[doc])
+                product + jnp.where(left, 0.0, value)
+                for product, value in zip(products, states[doc])
             ]
+    return states
+
+
+def finish_group(state, flat, out):
+    width, full = state.shape[2:]
+    left = lax.broadcasted_iota(jnp.int32, (width, full), 1) < width
+    states = [[state[doc, 0], state[doc, 1]] for doc in range(DOC_GROUP)]
+    states = newton_steps(states, left, NEWTON_STEPS - FIRST_STEPS)
     for doc in range(0, DOC_GROUP, 2):
         pair = (doc, doc + 1)
-        tilted = pair_product(
-            [states[d][0] for d in pair], [crossed[d] for d in pair], True)
+        tilted = pair_product([states[d][0] for d in pair], [state[d, 2] for d in pair], True)
         tilted = pair_product(tilted, [states[d][1] for d in pair], True)
         for d, value in zip(pair, tilted):
             flat[d * width:(d + 1) * width, :] = value
@@ -222,16 +236,18 @@
     return [
         pltpu.VMEM((full, total), BF16),
         pltpu.VMEM((1, total), jnp.int32),
+        pltpu.VMEM((DOC_GROUP, 3, full // 2, full), F32),
         pltpu.VMEM((DOC_GROUP * (full // 2), full), F32),
     ]
 
 
-def queries_kernel(recv_rows, recv_slot, out, turned, codes, flat):
+def queries_kernel(recv_rows, recv_slot, out, turned, codes, state, flat):
     prepare(recv_rows, recv_slot, turned, codes)
 
     @pl.loop(0, GROUPS)
     def _(step):
-        query_group(step, recv_rows, turned, codes, flat, out.at[step])
+        start_group(step, recv_rows, turned, codes, state)
+        finish_group(state, flat, out.at[step])
 
 
 def make_queries(recv_rows, recv_slot):
@@ -283,7 +299,7 @@
         copy(stop).wait_send()
 
 
-def grid_kernel(owners, recv_rows, recv_slot, train, out, turned, codes, flat, held,
+def grid_kernel(owners, recv_rows, recv_slot, train, out, turned, codes, state, flat, held,
                 up_sent, down_sent, side_sent, twin_sent, here):
     lines = owners // 4
     me = lax.axis_index("blk")
@@ -377,20 +393,9 @@
         for wish, sem, device, theirs in item[2]:
             when(wish, lambda: copy(group, item[0], sem, device, theirs).start())
 
-    @pl.loop(0, GROUPS + lines)
-    def _(step):
-        @pl.when(step < GROUPS)
-        def _():
-            query_group(step, recv_rows, turned, codes, flat, held.at[step, LEAD])
-
-            @pl.when(step == 0)
-            def _():
-                pl.semaphore_wait(barrier, 2 + has_up.astype(jnp.int32) + has_down.astype(jnp.int32))
-
-            hand_on(step, stages[0][0])
-
-        for stage in range(lines, 0, -1):
-            group = step - stage
+    def relay(step, stages_now):
+        for stage in stages_now:
+            group = step - (stage + 1) // 2
 
             @pl.when((group >= 0) & (group < GROUPS))
             def _():
@@ -398,15 +403,37 @@
                     when(item[1], lambda: arrive(group, item[0]))
                     hand_on(group, item)
 
-        @pl.when(step >= lines)
+    last = (lines + 1) // 2 + 1
+
+    @pl.loop(0, GROUPS + last)
+    def _(step):
+        @pl.when(step < GROUPS)
         def _():
-            group = step - lines
+            start_group(step, recv_rows, turned, codes, state)
+
+            @pl.when(step == 0)
+            def _():
+                pl.semaphore_wait(barrier, 2 + has_up.astype(jnp.int32) + has_down.astype(jnp.int32))
+
+        relay(step, [stage for stage in range(lines, 0, -1) if stage % 2 == 1])
+
+        @pl.when(step >= last)
+        def _():
+            group = step - last
             for items in stages:
                 for _, _, _, twin_stop, from_twin in items:
                     when(from_twin, lambda: arrive(group, twin_stop))
             block = held[group, :STOPS].reshape(STOPS * DOC_GROUP, train.shape[1])
             tile = lax.dot_general(block, train[...], CONTRACT_LAST, preferred_element_type=F32)
             out[group] = tile.astype(BF16).reshape(STOPS, DOC_GROUP, train.shape[0])
+
+        @pl.when(step < GROUPS)
+        def _():
+            finish_group(state, flat, held.at[step, LEAD])
+
+            hand_on(step, stages[0][0])
+
+        relay(step, [stage for stage in range(lines, 0, -1) if stage % 2 == 0])
 
     @pl.loop(0, GROUPS)
     def _(group):

time: 58.2 us -> 64 us (1.100)
  Pallas kernels: 55.6 us -> 61.4 us
    pallas_call x1, Pallas kernels: 40.7 us -> 46.5 us  [influence_of(): pl.pallas_call(functools.partial(grid_kernel, owners), out_shape=jax.Shap...]
where the time goes in v5:
time: 64 us; the launch traced here: 63 us
  Pallas kernels  61.4 us (96%)
  local copies, waits for them, and re-layouts  1.62 us (3%)
    pallas_call x1, Pallas kernels, influence_of(): pl.pallas_call(functools.partial(grid_kernel, owners), out_shape=jax.Shap...  46.5 us
    pallas_call x1, Pallas kernels, dispatch(): pl.pallas_call(functools.partial(dispatch_kernel, owners, capacity), out_...  14.9 us
    reshape x1, local copies, waits for them, and re-layouts, influence_of(): return tiles.transpose(1, 0, 2, 3).reshape(STOPS, DOC_DEV, train.shape[0])  1.62 us

profile of v5, /device:TPU:0, one launch (start us, length us, event | category | flops | bytes accessed | tf_op | source)
XLA Modules:
  0.0 63.0 jit_solution(9920506899033565995)
XLA Ops:
  0.0 14.9 %dispatch.1 = (bf16[16,64,128]{2,1,0:T(8,128)(2,1)}, s32[16,1,128]{2,1,0:T(1,128)}) custom-call(bf16[256,4096]{1,0:T(8,128)(2,1)} %x_in.1, bf16[256,4096]{1,0:T(8,128)(2,1)} %x_grad.1, bf16[64,4096]{1,0:T(8,128)(2,1)} %bitcast.9, bf16[64,4096]{1,0:T(8,128)(2,1)} %bitcast.10, s32[1,256]{1,0:T(1,128)} %bitcast.11, s32[1,256]{1,0:T(1,128)} %bitcast.12), custom_call_target="tpu_custom_call" | custom-call | tf_op jit(solution)/shard_map/dispatch/pallas_call | solution.py:136
  14.9 46.5 %influence.1 = bf16[4,12,8,256]{3,2,1,0:T(8,128)(2,1)} custom-call(bf16[16,64,128]{2,1,0:T(8,128)(2,1)} %get-tuple-element.7.recv_rows, s32[16,1,128]{2,1,0:T(1,128)} %get-tuple-element.8.recv_slot, bf16[256,4096]{1,0:T(8,128)(2,1)} %train.1), custom_call_target="tpu_custom_call" | custom-call | tf_op jit(solution)/shard_map/influence/pallas_call | solution.py:450
  61.4 1.6 %copy_bitcast_fusion = bf16[12,32,256]{2,1,0:T(8,128)(2,1)} fusion(bf16[4,12,8,256]{3,2,1,0:T(8,128)(2,1)} %influence.1), kind=kLoop, calls=%fused_computation | loop fusion | bytes 393216 | tf_op jit(solution)/shard_map/reshape | solution.py:461

commit v6 on v4

--- a/solution.py
+++ b/solution.py
@@ -54,10 +54,14 @@
     return product[:rows, :cols], product[rows:, cols:]
 
 
-def dispatch_kernel(owners, capacity, x_in, x_grad, p_in, p_out, owner_row, slot_row,
-                    recv_rows, recv_slot, low, send_rows, send_slot,
+def dispatch_kernel(owners, capacity, far_in, far_grad, p_in, p_out, owner_row, slot_row,
+                    recv_rows, recv_slot, x_in, x_grad, fetched, low, send_rows, send_slot,
                     rows_sent, rows_here, slot_sent, slot_here):
     me = lax.axis_index("blk")
+    fetch_grad = pltpu.make_async_copy(far_grad, x_grad, fetched.at[0])
+    fetch_in = pltpu.make_async_copy(far_in, x_in, fetched.at[1])
+    fetch_grad.start()
+    fetch_in.start()
     barrier = pltpu.get_barrier_semaphore()
 
     @pl.loop(1, owners)
@@ -68,10 +72,6 @@
 
     count = x_in.shape[0]
     width = p_in.shape[0]
-    for at, values, weights in ((0, x_grad, p_out), (width, x_in, p_in)):
-        low[:, at:at + width] = lax.dot_general(
-            values[...], weights[...], CONTRACT_LAST, preferred_element_type=F32
-        ).astype(BF16)
     token = lax.broadcasted_iota(jnp.int32, (count, count), 0)
     other = lax.broadcasted_iota(jnp.int32, (count, count), 1)
     earlier = jnp.where(token < other, 1.0, 0.0).astype(BF16)
@@ -82,6 +82,13 @@
     position = owner_row[...] * capacity + rank
     place = lax.broadcasted_iota(jnp.int32, (owners * capacity, count), 0)
     placed = jnp.where(place == position, 1.0, 0.0).astype(BF16)
+    for at, values, weights, fetch in (
+        (0, x_grad, p_out, fetch_grad), (width, x_in, p_in, fetch_in)
+    ):
+        fetch.wait()
+        low[:, at:at + width] = lax.dot_general(
+            values[...], weights[...], CONTRACT_LAST, preferred_element_type=F32
+        ).astype(BF16)
     send_rows[...] = matmul(placed, low[...]).astype(BF16).reshape(send_rows.shape)
     coded = jnp.where(owner_id == owner_row[...], slot_row[...] + 1, 0).astype(F32).astype(BF16)
     lane = lax.broadcasted_iota(jnp.int32, (LANES, count), 0)
@@ -135,9 +142,12 @@
     return pl.pallas_call(
         functools.partial(dispatch_kernel, owners, capacity),
         out_shape=(jax.ShapeDtypeStruct(rows, BF16), jax.ShapeDtypeStruct(slots, jnp.int32)),
-        in_specs=[VMEM_SPEC] * 6,
+        in_specs=[pl.BlockSpec(memory_space=pl.ANY)] * 2 + [VMEM_SPEC] * 4,
         out_specs=(VMEM_SPEC, VMEM_SPEC),
         scratch_shapes=[
+            pltpu.VMEM(x_in.shape, BF16),
+            pltpu.VMEM(x_in.shape, BF16),
+            pltpu.SemaphoreType.DMA((2,)),
             pltpu.VMEM((count, 2 * width), BF16),
             pltpu.VMEM(rows, BF16),
             pltpu.VMEM(slots, jnp.int32),
@@ -283,7 +293,7 @@
         copy(stop).wait_send()
 
 
-def grid_kernel(owners, recv_rows, recv_slot, train, out, turned, codes, flat, held,
+def grid_kernel(owners, recv_rows, recv_slot, train_far, out, turned, codes, flat, train, fetched, held,
                 up_sent, down_sent, side_sent, twin_sent, here):
     lines = owners // 4
     me = lax.axis_index("blk")
@@ -305,6 +315,8 @@
     greet(across)
     pl.when(has_up)(lambda: greet(above))
     pl.when(has_down)(lambda: greet(below))
+    fetch = pltpu.make_async_copy(train_far, train, fetched)
+    fetch.start()
     prepare(recv_rows, recv_slot, turned, codes)
 
     def wrapped(stop):
@@ -404,6 +416,7 @@
             for items in stages:
                 for _, _, _, twin_stop, from_twin in items:
                     when(from_twin, lambda: arrive(group, twin_stop))
+            pl.when(group == 0)(fetch.wait)
             block = held[group, :STOPS].reshape(STOPS * DOC_GROUP, train.shape[1])
             tile = lax.dot_general(block, train[...], CONTRACT_LAST, preferred_element_type=F32)
             out[group] = tile.astype(BF16).reshape(STOPS, DOC_GROUP, train.shape[0])
@@ -423,9 +436,10 @@
         tiles = pl.pallas_call(
             functools.partial(grid_kernel, owners),
             out_shape=jax.ShapeDtypeStruct((GROUPS, STOPS, DOC_GROUP, train.shape[0]), BF16),
-            in_specs=[VMEM_SPEC] * 3,
+            in_specs=[VMEM_SPEC, VMEM_SPEC, pl.BlockSpec(memory_space=pl.ANY)],
             out_specs=VMEM_SPEC,
             scratch_shapes=query_scratch(recv_rows)
+            + [pltpu.VMEM(train.shape, BF16), pltpu.SemaphoreType.DMA]
             + [pltpu.VMEM((GROUPS, owners, DOC_GROUP, train.shape[1]), BF16)]
             + [pltpu.SemaphoreType.DMA((GROUPS, owners))] * 5,
             compiler_params=params,

time: 58.2 us -> 58.1 us (level)
    pallas_call x1, Pallas kernels: 40.7 us -> 39 us  [influence_of(): pl.pallas_call(functools.partial(grid_kernel, owners), out_shape=jax.Shap...]
    pallas_call x1, Pallas kernels: 14.9 us -> 16.4 us  [dispatch(): pl.pallas_call(functools.partial(dispatch_kernel, owners, capacity), out_...]
where the time goes in v6:
time: 58.1 us; the launch traced here: 57.1 us
  Pallas kernels  55.5 us (96%)
  local copies, waits for them, and re-layouts  1.62 us (3%)
    pallas_call x1, Pallas kernels, influence_of(): pl.pallas_call(functools.partial(grid_kernel, owners), out_shape=jax.Shap...  39 us
    pallas_call x1, Pallas kernels, dispatch(): pl.pallas_call(functools.partial(dispatch_kernel, owners, capacity), out_...  16.4 us
    reshape x1, local copies, waits for them, and re-layouts, influence_of(): return tiles.transpose(1, 0, 2, 3).reshape(STOPS, DOC_DEV, train.shape[0])  1.62 us

profile of v6, /device:TPU:0, one launch (start us, length us, event | category | flops | bytes accessed | tf_op | source)
XLA Modules:
  0.0 57.1 jit_solution(1357141355935695905)
XLA Ops:
  0.0 16.4 %dispatch.1 = (bf16[16,64,128]{2,1,0:T(8,128)(2,1)}, s32[16,1,128]{2,1,0:T(1,128)}) custom-call(bf16[256,4096]{1,0:T(8,128)(2,1)} %far_in.1, bf16[256,4096]{1,0:T(8,128)(2,1)} %far_grad.1, bf16[64,4096]{1,0:T(8,128)(2,1)} %bitcast.9, bf16[64,4096]{1,0:T(8,128)(2,1)} %bitcast.10, s32[1,256]{1,0:T(1,128)} %bitcast.11, s32[1,256]{1,0:T(1,128)} %bitcast.12), custom_call_target="tpu_custom_call" | custom-call | tf_op jit(solution)/shard_map/dispatch/pallas_call | solution.py:142
  16.5 39.0 %influence.1 = bf16[4,12,8,256]{3,2,1,0:T(8,128)(2,1)} custom-call(bf16[16,64,128]{2,1,0:T(8,128)(2,1)} %get-tuple-element.7.recv_rows, s32[16,1,128]{2,1,0:T(1,128)} %get-tuple-element.8.recv_slot, bf16[256,4096]{1,0:T(8,128)(2,1)} %train_far.1), custom_call_target="tpu_custom_call" | custom-call | tf_op jit(solution)/shard_map/influence/pallas_call | solution.py:436
  55.5 1.6 %copy_bitcast_fusion = bf16[12,32,256]{2,1,0:T(8,128)(2,1)} fusion(bf16[4,12,8,256]{3,2,1,0:T(8,128)(2,1)} %influence.1), kind=kLoop, calls=%fused_computation | loop fusion | bytes 393216 | tf_op jit(solution)/shard_map/reshape | solution.py:448

commit v7 on v4

--- a/solution.py
+++ b/solution.py
@@ -12,7 +12,7 @@
 NEWTON_STEPS = 6
 LEAD = 5
 LANES = 128
-DOC_GROUP = 8
+DOC_GROUP = 4
 GROUPS = DOC_DEV // DOC_GROUP
 MESH = pl.DeviceIdType.MESH
 VMEM_SPEC = pl.BlockSpec(memory_space=pltpu.VMEM)

time: 58.2 us -> 71.2 us (1.22)
  Pallas kernels: 55.6 us -> 68.5 us
    pallas_call x1, Pallas kernels: 40.7 us -> 53.6 us  [influence_of(): pl.pallas_call(functools.partial(grid_kernel, owners), out_shape=jax.Shap...]
    transpose x0 -> x1, local copies, waits for them, and re-layouts: none -> 1.01 us  [influence_of(): return tiles.transpose(1, 0, 2, 3).reshape(STOPS, DOC_DEV, train.shape[0])]
    reshape x1, local copies, waits for them, and re-layouts: 1.62 us -> 0.73 us  [influence_of(): return tiles.transpose(1, 0, 2, 3).reshape(STOPS, DOC_DEV, train.shape[0])]
where the time goes in v7:
time: 71.2 us; the launch traced here: 70.3 us
  Pallas kernels  68.5 us (96%)
  local copies, waits for them, and re-layouts  1.74 us (2%)
    pallas_call x1, Pallas kernels, influence_of(): pl.pallas_call(functools.partial(grid_kernel, owners), out_shape=jax.Shap...  53.6 us
    pallas_call x1, Pallas kernels, dispatch(): pl.pallas_call(functools.partial(dispatch_kernel, owners, capacity), out_...  14.9 us

profile of v7, /device:TPU:0, one launch (start us, length us, event | category | flops | bytes accessed | tf_op | source)
XLA Modules:
  0.0 70.3 jit_solution(5598558090865684834)
XLA Ops:
  0.0 14.9 %dispatch.1 = (bf16[16,64,128]{2,1,0:T(8,128)(2,1)}, s32[16,1,128]{2,1,0:T(1,128)}) custom-call(bf16[256,4096]{1,0:T(8,128)(2,1)} %x_in.1, bf16[256,4096]{1,0:T(8,128)(2,1)} %x_grad.1, bf16[64,4096]{1,0:T(8,128)(2,1)} %bitcast.6, bf16[64,4096]{1,0:T(8,128)(2,1)} %bitcast.7, s32[1,256]{1,0:T(1,128)} %bitcast.8, s32[1,256]{1,0:T(1,128)} %bitcast.9), custom_call_target="tpu_custom_call" | custom-call | tf_op jit(solution)/shard_map/dispatch/pallas_call | solution.py:135
  14.9 53.6 %influence.1 = bf16[8,12,4,256]{3,2,1,0:T(4,128)(2,1)} custom-call(bf16[16,64,128]{2,1,0:T(8,128)(2,1)} %get-tuple-element.7.recv_rows, s32[16,1,128]{2,1,0:T(1,128)} %get-tuple-element.8.recv_slot, bf16[256,4096]{1,0:T(8,128)(2,1)} %train.1), custom_call_target="tpu_custom_call" | custom-call | tf_op jit(solution)/shard_map/influence/pallas_call | solution.py:423
  68.6 1.0 %copy.8 = bf16[12,8,4,256]{3,2,1,0:T(4,128)(2,1)S(1)} copy(bf16[12,8,4,256]{3,2,0,1:T(4,128)(2,1)} %bitcast.5) | data formatting | bytes 393216 | tf_op jit(solution)/shard_map/transpose | solution.py:434
  69.6 0.7 %reshape.11 = bf16[12,32,256]{2,1,0:T(8,128)(2,1)} reshape(bf16[12,8,4,256]{3,2,1,0:T(4,128)(2,1)S(1)} %copy.8) | data formatting | bytes 393216 | tf_op jit(solution)/shard_map/reshape | solution.py:434
